TPU v7x, 128 devices: a whole 4x4x4 slice. The times are simulated.
128 devices in a mesh: rhs: 4 (over y), rows: 32 (over x, z, core).
Axes of the slice: x: 4, y: 4, z: 4, core: 2. Of those that a mesh axis runs over, the one named last changes fastest.
Arguments:
- right_side: float32 [65536, 512], P('rows', 'rhs'), may hold values from -6 to 6
- fine_blocks: bfloat16 [512, 32, 128, 128], P('rows'), may hold values from -0.09375 to 0.09375
- fine_columns: int32 [512, 32], P('rows'), may hold values from 0 to 511, as said below
- fine_diag: float32 [65536], P('rows'), may hold values from 3 to 6
- aggregate: int32 [512], P('rows'), may hold values from 0 to 127, as said below
- coarse_blocks: float32 [128, 3, 128, 128], P(('rhs', 'rows')), may hold values from -0.3125 to 0.3125
- coarse_diag: float32 [16384], P(('rhs', 'rows')), may hold values from 1 to 2
Outputs:
- solution: float32 [65536, 512], P('rows', 'rhs')
Inputs may be any that keep to these rules, and one draw needn't show every extreme that they name: `fine_columns`: the 32 stored blocks of fine block-row r have 32 distinct columns, each equal to r + o modulo 512 for an offset o from -16 to 16, and every row holds both end offsets. `aggregate`: fine block-row r maps to a coarse block c with c % (32) equal to r // 16; every coarse block receives one or more fine block-rows.
All inputs are finite; a program needn't handle non-finite values.
Results may differ from a plain program's by a relative error of at most 0.004.
Values may be sent and summed in bfloat16 or wider, within the bound.
No kernel may reach another device: no remote copies, remote signals or barrier semaphores. Data moves between devices by JAX's collectives and lax.ppermute only.
A program may use at most 128 MiB of HBM per device.

v0:
```python
import jax
import jax.numpy as jnp
from jax import lax
from jax.experimental import pallas as pl
from jax.experimental.pallas import tpu as pltpu
from jax.sharding import PartitionSpec as P

CYCLES = 2
CHEB = 3
RELAX = 0.7
THETA = 1.0
DELTA = 0.6

B = 128
ROWS = 16
GROUP = 4
TILE = GROUP * B
TILE_ROWS = ROWS // GROUP
SLOTS = 36
FIELD = ROWS * B
TAIL = 16
QROWS = 4 * B

f32 = jnp.float32
bf16 = jnp.bfloat16
VMEM_SPEC = pl.BlockSpec(memory_space=pltpu.VMEM)
SMEM_SPEC = pl.BlockSpec(memory_space=pltpu.SMEM)
ANY_SPEC = pl.BlockSpec(memory_space=pl.ANY)
LIMIT = 12 * 1024 * 1024


def resident(x):
    return pltpu.with_memory_space_constraint(x, pltpu.VMEM)


def core_of():
    return lax.rem(lax.axis_index("rows"), 2)


def column(row):
    return jnp.transpose(jnp.broadcast_to(row, (B, B)))


def start_kernel(
    right_ref, diag_ref, group_ref, first_ref, sent_ref, ratio_ref, diag_out_ref, right_s, diag_s, group_s, sems
):
    chunks = [
        pltpu.make_async_copy(
            right_ref.at[pl.ds(g * TILE, TILE), :], right_s.at[pl.ds(g * TILE, TILE), :], sems.at[g]
        )
        for g in range(TILE_ROWS)
    ]
    diag_copy = pltpu.make_async_copy(diag_ref, diag_s, sems.at[TILE_ROWS])
    group_copy = pltpu.make_async_copy(group_ref, group_s, sems.at[TILE_ROWS + 1])
    diag_copy.start()
    for chunk in chunks:
        chunk.start()
    group_copy.start()
    diag_copy.wait()
    for g in range(TILE_ROWS):
        chunks[g].wait()
        for r in range(g * GROUP, (g + 1) * GROUP):
            rows = pl.ds(r * B, B)
            diag = column(diag_s[r : r + 1, :])
            ratio = RELAX / diag
            value = ratio * right_s[rows, :]
            diag_out_ref[rows, :] = diag
            ratio_ref[rows, :] = ratio
            first_ref[rows, :] = value
            sent_ref[rows, :] = value.astype(bf16)
    group_copy.wait()
    size = lax.axis_size("rows")
    index = lax.broadcasted_iota(jnp.int32, (TAIL, B), 0)
    tail = jnp.zeros((TAIL, B), f32)
    for r in range(ROWS):
        tail = jnp.where(index == r, lax.div(group_s[r], size).astype(f32), tail)
    sent_ref[pl.ds(FIELD, TAIL), :] = tail.astype(bf16)


def pack_kernel(blocks_ref, diag_ref, out_ref):
    inverse = 1.0 / diag_ref[...]
    scale = column(inverse)
    for d in range(3):
        out_ref[pl.ds(d * B, B), :] = (scale * blocks_ref[0, d]).astype(bf16)
    high = inverse.astype(bf16).astype(f32)
    low = inverse - high
    index = lax.broadcasted_iota(jnp.int32, (TAIL, B), 0)
    out_ref[pl.ds(3 * B, TAIL), :] = jnp.where(index == 0, high, low).astype(bf16)


def sort_kernel(p0_ref, p1_ref, p2_ref, p3_ref, after_ref, ops_ref, scale_ref):
    me = lax.axis_index("rhs")
    for k, ref in enumerate((p0_ref, p1_ref, p2_ref, p3_ref)):
        q = jnp.bitwise_and(me - k + 4, 3)
        for d in range(3):
            ops_ref[q * 3 + d] = ref[pl.ds(d * B, B), :]
        tail = ref[pl.ds(3 * B, TAIL), :].astype(f32)
        scale_ref[pl.ds(q * B, B), :] = column(tail[0:1, :] + tail[1:2, :])


def tile_product(kept_ref, group, slot, count, field):
    lhs = jnp.concatenate(
        [
            jnp.concatenate(
                [kept_ref[(group * GROUP + a) * SLOTS + slot + b] for b in range(GROUP * count)],
                axis=1,
            )
            for a in range(GROUP)
        ],
        axis=0,
    )
    return jnp.dot(lhs, field, preferred_element_type=f32)


def side_product(kept_ref, upper, m, field_ref):
    group = jnp.where(upper, m, TILE_ROWS - 1 - m)
    start = pl.multiple_of(jnp.where(upper, 0, TILE * (TILE_ROWS - 1 - m)), TILE)
    slot = jnp.where(upper, GROUP * (2 * TILE_ROWS - m), 0)
    field = field_ref[pl.ds(start, TILE * (m + 1)), :]
    return group, tile_product(kept_ref, group, slot, m + 1, field)


def near_products(kept_ref, own_ref, near_ref, first, second, ready=None):
    @pl.loop(0, TILE_ROWS)
    def _(group):
        if ready is not None:
            ready(group)
        part = tile_product(
            kept_ref, group, GROUP * (TILE_ROWS - group), TILE_ROWS, own_ref[pl.ds(0, FIELD), :]
        )
        first(pl.ds(pl.multiple_of(group * TILE, TILE), TILE), part)

    upper = core_of() == 0
    for m in range(TILE_ROWS):
        group, part = side_product(kept_ref, upper, m, near_ref)
        second(pl.ds(pl.multiple_of(group * TILE, TILE), TILE), part)


def far_products(kept_ref, far_ref, emit):
    upper = core_of() == 1
    for m in range(TILE_ROWS):
        group, part = side_product(kept_ref, upper, m, far_ref)
        emit(pl.ds(pl.multiple_of(group * TILE, TILE), TILE), part)


def sweep_near(kept_ref, own_ref, near_ref, x_ref, first_ref, ratio_ref, base_ref, ready=None):
    def first(rows, part):
        base_ref[rows, :] = (1.0 - RELAX) * x_ref[rows, :] + first_ref[rows, :] - ratio_ref[rows, :] * part

    def second(rows, part):
        base_ref[rows, :] -= ratio_ref[rows, :] * part

    near_products(kept_ref, own_ref, near_ref, first, second, ready)


def sweep_near_kernel(kept_ref, own_ref, near_ref, x_ref, first_ref, ratio_ref, base_ref):
    sweep_near(kept_ref, own_ref, near_ref, x_ref, first_ref, ratio_ref, base_ref)


def load_near_kernel(
    columns_ref, blocks_ref, own_ref, near_ref, x_ref, first_ref, ratio_ref, kept_ref, base_ref, sems
):
    first = lax.axis_index("rows") * ROWS - ROWS
    empty = jnp.zeros((B, B), bf16)

    @pl.loop(0, ROWS)
    def _(r):
        lead = lax.rem(r, GROUP)
        sem = sems.at[lax.div(r, GROUP)]
        base = r * SLOTS
        total = jnp.int32(0)
        for k in range(2 * ROWS):
            offset = jnp.bitwise_and(columns_ref[r, k] - first - r + 512, 511)
            offset = jnp.minimum(offset, 2 * ROWS)
            pltpu.make_async_copy(blocks_ref.at[r, k], kept_ref.at[base + lead + offset], sem).start()
            total = total + offset
        missing = jnp.clip(ROWS * (2 * ROWS + 1) - total, 0, 2 * ROWS)
        kept_ref[base + lead + missing] = empty
        for pad in range(GROUP - 1):
            place = jnp.where(pad < lead, pad, 2 * ROWS + 1 + pad)
            kept_ref[base + place] = empty

    def ready(group):
        for a in range(GROUP):
            r = group * GROUP + a
            pltpu.make_async_copy(
                blocks_ref.at[r], kept_ref.at[pl.ds(r * 2 * ROWS, 2 * ROWS)], sems.at[group]
            ).wait()

    sweep_near(kept_ref, own_ref, near_ref, x_ref, first_ref, ratio_ref, base_ref, ready)


def sweep_far_kernel(kept_ref, far_ref, base_ref, ratio_ref, x_ref, sent_ref):
    def emit(rows, part):
        value = base_ref[rows, :] - ratio_ref[rows, :] * part
        x_ref[rows, :] = value
        sent_ref[rows, :] = value.astype(bf16)

    far_products(kept_ref, far_ref, emit)


def last_far_kernel(kept_ref, far_ref, base_ref, ratio_ref, x_ref, x_s, sems):
    copies = []

    def emit(rows, part):
        x_s[rows, :] = base_ref[rows, :] - ratio_ref[rows, :] * part
        copy = pltpu.make_async_copy(x_s.at[rows, :], x_ref.at[rows, :], sems.at[len(copies)])
        copy.start()
        copies.append(copy)

    far_products(kept_ref, far_ref, emit)
    for copy in copies:
        copy.wait()


def residual_near_kernel(kept_ref, own_ref, near_ref, x_ref, right_ref, diag_ref, base_ref):
    def first(rows, part):
        base_ref[rows, :] = right_ref[rows, :] - diag_ref[rows, :] * x_ref[rows, :] - part

    def second(rows, part):
        base_ref[rows, :] -= part

    near_products(kept_ref, own_ref, near_ref, first, second)


def residual_far_kernel(kept_ref, group_ref, far_ref, base_ref, scale_ref, res_ref, side_ref, sent_ref):
    def emit(rows, part):
        res_ref[rows, :] = base_ref[rows, :] - part

    far_products(kept_ref, far_ref, emit)
    side_ref[...] = jnp.zeros((QROWS, B), f32)
    for r in range(ROWS):
        rows = pl.ds(pl.multiple_of(lax.div(group_ref[r], lax.axis_size("rows")) * B, B), B)
        side_ref[rows, :] += res_ref[pl.ds(r * B, B), :]
    value = scale_ref[...] * side_ref[...]
    side_ref[...] = value
    sent_ref[...] = value.astype(bf16)


def spread(coarse_ref, tail_ref, out_ref):
    tail = tail_ref[pl.ds(FIELD, TAIL), :].astype(f32)
    parts = [coarse_ref[pl.ds(q * B, B), :].astype(f32) for q in range(4)]
    for r in range(ROWS):
        group = tail[r : r + 1, :]
        value = jnp.where(group < 0.5, parts[0], parts[1])
        value = jnp.where(group < 1.5, value, parts[2])
        value = jnp.where(group < 2.5, value, parts[3])
        out_ref[pl.ds(r * B, B), :] = value.astype(bf16)


def lift_near_kernel(
    kept_ref, group_ref, coarse_ref, near_ref, near_tail_ref, x_ref, res_ref, ratio_ref, base_ref, own_s, near_s
):
    for r in range(ROWS):
        rows = pl.ds(pl.multiple_of(lax.div(group_ref[r], lax.axis_size("rows")) * B, B), B)
        own_s[pl.ds(r * B, B), :] = coarse_ref[rows, :]
    spread(near_ref, near_tail_ref, near_s)

    def first(rows, part):
        base_ref[rows, :] = (
            x_ref[rows, :]
            + (1.0 - RELAX) * own_s[rows, :].astype(f32)
            + ratio_ref[rows, :] * (res_ref[rows, :] - part)
        )

    def second(rows, part):
        base_ref[rows, :] -= ratio_ref[rows, :] * part

    near_products(kept_ref, own_s, near_s, first, second)


def lift_far_kernel(kept_ref, far_ref, far_tail_ref, base_ref, ratio_ref, x_ref, sent_ref, far_s):
    spread(far_ref, far_tail_ref, far_s)
    sweep_far_kernel(kept_ref, far_s, base_ref, ratio_ref, x_ref, sent_ref)


def coarse_terms(ops_ref, own_ref, near_ref, far_ref, emit):
    i = lax.axis_index("rows")
    last = lax.axis_size("rows") - 1
    near_is_upper = (core_of() == 0).astype(f32)
    step_up = (i == last).astype(jnp.int32)
    step_down = (i == 0).astype(jnp.int32)
    for q in range(4):
        at_up = pl.multiple_of(jnp.minimum(q + step_up, 3) * B, B)
        at_down = pl.multiple_of(jnp.maximum(q - step_down, 0) * B, B)
        keep_up = (q + step_up <= 3).astype(f32)
        keep_down = (q - step_down >= 0).astype(f32)
        upper = near_is_upper * near_ref[pl.ds(at_up, B), :].astype(f32) + (
            1.0 - near_is_upper
        ) * far_ref[pl.ds(at_up, B), :].astype(f32)
        lower = near_is_upper * far_ref[pl.ds(at_down, B), :].astype(f32) + (
            1.0 - near_is_upper
        ) * near_ref[pl.ds(at_down, B), :].astype(f32)
        field = jnp.concatenate(
            [
                (keep_down * lower).astype(bf16),
                own_ref[pl.ds(q * B, B), :],
                (keep_up * upper).astype(bf16),
            ],
            axis=0,
        )
        ops = jnp.concatenate([ops_ref[q * 3 + d] for d in range(3)], axis=1)
        emit(pl.ds(q * B, B), jnp.dot(ops, field, preferred_element_type=f32))


def ratios():
    sigma = THETA / DELTA
    old = 1.0 / sigma
    out = []
    for _ in range(CHEB - 1):
        new = 1.0 / (2.0 * sigma - old)
        out.append((new * old, 2.0 * new / DELTA))
        old = new
    return out


def coarse_first_kernel(ops_ref, side_ref, own_ref, near_ref, far_ref, fix_ref, sent_ref):
    keep, gain = ratios()[0]

    def emit(rows, part):
        side = side_ref[rows, :] / THETA
        fix = side + keep * side + gain * (side_ref[rows, :] - side - part)
        fix_ref[rows, :] = fix
        sent_ref[rows, :] = fix.astype(bf16)

    coarse_terms(ops_ref, own_ref, near_ref, far_ref, emit)


def coarse_second_kernel(ops_ref, side_ref, fix_ref, own_ref, near_ref, far_ref, sent_ref):
    keep, gain = ratios()[1]

    def emit(rows, part):
        fix = fix_ref[rows, :]
        update = fix - side_ref[rows, :] / THETA
        fix = fix + keep * update + gain * (side_ref[rows, :] - fix - part)
        sent_ref[rows, :] = fix.astype(bf16)

    coarse_terms(ops_ref, own_ref, near_ref, far_ref, emit)


def run(kernel, outs, args, scratch=(), cost=(0, 0), to_hbm=False):
    specs, values = [], []
    for value, space in args:
        if space == "v":
            specs.append(VMEM_SPEC)
            values.append(resident(value))
        elif space == "b":
            specs.append(VMEM_SPEC)
            values.append(value)
        elif space == "s":
            specs.append(SMEM_SPEC)
            values.append(value)
        else:
            specs.append(ANY_SPEC)
            values.append(pltpu.with_memory_space_constraint(value, pltpu.HBM))
    return pl.pallas_call(
        kernel,
        out_shape=[
            jax.ShapeDtypeStruct(shape, dtype) if to_hbm else pltpu.VMEM(shape, dtype)
            for shape, dtype in outs
        ],
        in_specs=specs,
        out_specs=[ANY_SPEC if to_hbm else VMEM_SPEC] * len(outs),
        scratch_shapes=list(scratch),
        cost_estimate=pl.CostEstimate(flops=cost[0], bytes_accessed=cost[1], transcendentals=0),
        compiler_params=pltpu.CompilerParams(vmem_limit_bytes=LIMIT),
    )(*values)


def swap(x, size):
    far = lax.ppermute(
        x, "rows", [(i, (i - 1) % size if i % 2 == 0 else (i + 1) % size) for i in range(size)]
    )
    near = lax.ppermute(x, "rows", [(i, i ^ 1) for i in range(size)])
    return near, far


FULL = (FIELD, B)
SIDE = (QROWS, B)
NEAR_COST = (2 * 26 * TILE * TILE * B, 8_000_000)
FAR_COST = (2 * 10 * TILE * TILE * B, 3_000_000)


def shards(right_side, fine_blocks, fine_columns, fine_diag, aggregate, coarse_blocks, coarse_diag):
    size = lax.axis_size("rows")
    group = aggregate

    first, sent, ratio, diag = run(
        start_kernel,
        [(FULL, f32), ((FIELD + TAIL, B), bf16), (FULL, f32), (FULL, f32)],
        [(right_side, "h"), (fine_diag.reshape(ROWS, B), "h"), (group, "h")],
        [
            pltpu.VMEM(FULL, f32),
            pltpu.VMEM((ROWS, B), f32),
            pltpu.SMEM((ROWS,), jnp.int32),
            pltpu.SemaphoreType.DMA((TILE_ROWS + 2,)),
        ],
    )
    near, far = swap(sent, size)
    near_tail, far_tail = near, far
    kept, base = run(
        load_near_kernel,
        [((ROWS * SLOTS, B, B), bf16), (FULL, f32)],
        [
            (fine_columns, "s"), (fine_blocks, "h"), (sent, "v"), (near, "v"), (first, "v"),
            (first, "v"), (ratio, "v"),
        ],
        [pltpu.SemaphoreType.DMA((TILE_ROWS,))],
        (NEAR_COST[0], 28_000_000),
    )
    (packed,) = run(
        pack_kernel,
        [((3 * B + TAIL, B), bf16)],
        [(coarse_blocks, "b"), (coarse_diag.reshape(1, B), "b")],
    )
    pieces = [packed] + [
        lax.ppermute(packed, "rhs", [(i, (i + k) % 4) for i in range(4)]) for k in range(1, 4)
    ]
    def sweep_start(x, sent, near):
        return run(
            sweep_near_kernel,
            [(FULL, f32)],
            [(kept, "v"), (sent, "v"), (near, "v"), (x, "v"), (first, "v"), (ratio, "v")],
            cost=NEAR_COST,
        )[0]

    def sweep_end(far, base):
        return run(
            sweep_far_kernel,
            [(FULL, f32), (FULL, bf16)],
            [(kept, "v"), (far, "v"), (base, "v"), (ratio, "v")],
            cost=FAR_COST,
        )

    x = first
    for turn in range(CYCLES):
        for _ in range(2 * (turn > 0)):
            near, far = swap(sent, size)
            base = sweep_start(x, sent, near)
            x, sent = sweep_end(far, base)
        if turn == 0:
            x, sent = sweep_end(far, base)
        near, far = swap(sent, size)
        (base,) = run(
            residual_near_kernel,
            [(FULL, f32)],
            [(kept, "v"), (sent, "v"), (near, "v"), (x, "v"), (right_side, "b"), (diag, "v")],
            cost=NEAR_COST,
        )
        if turn == 0:
            ops, scale = run(
                sort_kernel,
                [((12, B, B), bf16), (SIDE, f32)],
                [(p, "v") for p in pieces] + [(base, "v")],
            )
        res, side, sent = run(
            residual_far_kernel,
            [(FULL, f32), (SIDE, f32), (SIDE, bf16)],
            [(kept, "v"), (group, "s"), (far, "v"), (base, "v"), (scale, "v")],
            cost=FAR_COST,
        )
        near, far = swap(sent, size)
        fix, sent = run(
            coarse_first_kernel,
            [(SIDE, f32), (SIDE, bf16)],
            [(ops, "v"), (side, "v"), (sent, "v"), (near, "v"), (far, "v")],
        )
        near, far = swap(sent, size)
        (sent,) = run(
            coarse_second_kernel,
            [(SIDE, bf16)],
            [(ops, "v"), (side, "v"), (fix, "v"), (sent, "v"), (near, "v"), (far, "v")],
        )
        near, far = swap(sent, size)
        (base,) = run(
            lift_near_kernel,
            [(FULL, f32)],
            [
                (kept, "v"), (group, "s"), (sent, "v"), (near, "v"), (near_tail, "v"),
                (x, "v"), (res, "v"), (ratio, "v"),
            ],
            [pltpu.VMEM(FULL, bf16), pltpu.VMEM(FULL, bf16)],
            NEAR_COST,
        )
        x, sent = run(
            lift_far_kernel,
            [(FULL, f32), (FULL, bf16)],
            [(kept, "v"), (far, "v"), (far_tail, "v"), (base, "v"), (ratio, "v")],
            [pltpu.VMEM(FULL, bf16)],
            FAR_COST,
        )
        near, far = swap(sent, size)
        base = sweep_start(x, sent, near)
        if turn < CYCLES - 1:
            x, sent = sweep_end(far, base)
    (x,) = run(
        last_far_kernel,
        [(FULL, f32)],
        [(kept, "v"), (far, "v"), (base, "v"), (ratio, "v")],
        [pltpu.VMEM(FULL, f32), pltpu.SemaphoreType.DMA((TILE_ROWS,))],
        FAR_COST,
        to_hbm=True,
    )
    return x


def solution(mesh):
    in_specs = (
        P("rows", "rhs"),
        P("rows", None, None, None),
        P("rows", None),
        P("rows"),
        P("rows"),
        P(("rhs", "rows"), None, None, None),
        P(("rhs", "rows")),
    )
    return jax.shard_map(
        shards, mesh=mesh, in_specs=in_specs, out_specs=P("rows", "rhs"), check_vma=False
    )
```

profile of v0, /device:TPU:0, one launch (start us, length us, event | category | flops | bytes accessed | tf_op | source)
XLA Modules:
  0.0 156.9 jit_solution(8117196869654876785)
XLA Ops:
  1.7 6.4 %collective-permute-start.4 = (bf16[2064,128]{1,0:T(8,128)(2,1)S(1)}, bf16[2064,128]{1,0:T(8,128)(2,1)S(1)}, u32[]{:S(2)}, u32[]{:S(2)}) collective-permute-start(bf16[2064,128]{1,0:T(8,128)(2,1)S(1)} %get-tuple-element.35.own_ref), channel_id=1, source_target_pairs={{0,31},{1,2},{2,1},{3,4},{4,3},{5,6},{6,5},{7,8},{8,7},{9,10},{10,... | collective-permute-start | bytes 1585160 | tf_op jit(solution)/shard_map/ppermute | solution.py:371
  8.9 8.7 %shard_map.74 = (bf16[576,128,128]{2,1,0:T(8,128)(2,1)S(1)}, f32[2048,128]{1,0:T(8,128)S(1)}) custom-call(s32[16,32]{1,0:T(8,128)S(1)} %copy-done.3, bf16[16,32,128,128]{3,2,1,0:T(8,128)(2,1)} %blocks_ref.2, bf16[2064,128]{1,0:T(8,128)(2,1)S(1)} %get-tuple-element.35.own_ref, bf16[2064,128]{1,0:T(8,128)(2,1)S(1)} %collective-permute-done.near_ref.near_tail_ref, ...), custom_call_target="tpu_custom_call" | custom-call | flops 1744830464 | bytes 28000000 | tf_op jit(solution)/shard_map/pallas_call | solution.py:356
  22.0 3.1 %collective-permute-start.3 = (bf16[400,128]{1,0:T(8,128)(2,1)S(1)}, bf16[400,128]{1,0:T(8,128)(2,1)S(1)}, u32[]{:S(2)}, u32[]{:S(2)}) collective-permute-start(bf16[400,128]{1,0:T(8,128)(2,1)S(1)} %shard_map.75.p0_ref), channel_id=1, source_target_pairs={{0,96},{32,0},{64,32},{96,64},{1,97},{33,1},{65,33},{97,65},{2,98}... | collective-permute-start | bytes 307208 | tf_op jit(solution)/shard_map/ppermute | solution.py:417
  26.7 4.4 %shard_map.77.after_ref.base_ref = f32[2048,128]{1,0:T(8,128)S(1)} custom-call(bf16[576,128,128]{2,1,0:T(8,128)(2,1)S(1)} %get-tuple-element.38.kept_ref, bf16[2048,128]{1,0:T(8,128)(2,1)S(1)} %get-tuple-element.40.own_ref, bf16[2048,128]{1,0:T(8,128)(2,1)S(1)} %collective-permute-done.5.near_ref, f32[2048,128]{1,0:T(8,128)S(1)} %get-tuple-element.41.x_ref, ...), custom_call_target="tpu_custom_call" | custom-call | flops 1744830464 | bytes 8000000 | tf_op jit(solution)/shard_map/pallas_call | solution.py:356
  36.8 5.8 %collective-permute-done.8.far_ref = bf16[512,128]{1,0:T(8,128)(2,1)S(1)} collective-permute-done((bf16[512,128]{1,0:T(8,128)(2,1)S(1)}, bf16[512,128]{1,0:T(8,128)(2,1)S(1)}, u32[]{:S(2)}, u32[]{:S(2)}) %collective-permute-start.8) | collective-permute-done | bytes 131104 | tf_op jit(solution)/shard_map/ppermute | solution.py:371
  44.9 5.8 %collective-permute-done.10.far_ref = bf16[512,128]{1,0:T(8,128)(2,1)S(1)} collective-permute-done((bf16[512,128]{1,0:T(8,128)(2,1)S(1)}, bf16[512,128]{1,0:T(8,128)(2,1)S(1)}, u32[]{:S(2)}, u32[]{:S(2)}) %collective-permute-start.10) | collective-permute-done | bytes 131104 | tf_op jit(solution)/shard_map/ppermute | solution.py:371
  53.2 5.2 %shard_map.82.base_ref = f32[2048,128]{1,0:T(8,128)S(1)} custom-call(bf16[576,128,128]{2,1,0:T(8,128)(2,1)S(1)} %get-tuple-element.38.kept_ref, s32[16]{0:T(128)S(1)} %copy-done.2, bf16[512,128]{1,0:T(8,128)(2,1)S(1)} %shard_map.81.coarse_ref, bf16[512,128]{1,0:T(8,128)(2,1)S(1)} %collective-permute-done.12.near_ref, ...), custom_call_target="tpu_custom_call" | custom-call | flops 1744830464 | bytes 8000000 | tf_op jit(solution)/shard_map/pallas_call | solution.py:356
  63.4 4.4 %shard_map.84.base_ref = f32[2048,128]{1,0:T(8,128)S(1)} custom-call(bf16[576,128,128]{2,1,0:T(8,128)(2,1)S(1)} %get-tuple-element.38.kept_ref, bf16[2048,128]{1,0:T(8,128)(2,1)S(1)} %get-tuple-element.50.own_ref, bf16[2048,128]{1,0:T(8,128)(2,1)S(1)} %collective-permute-done.14.near_ref, f32[2048,128]{1,0:T(8,128)S(1)} %get-tuple-element.51.x_ref, ...), custom_call_target="tpu_custom_call" | custom-call | flops 1744830464 | bytes 8000000 | tf_op jit(solution)/shard_map/pallas_call | solution.py:356
  67.9 4.9 %collective-permute-done.13.far_ref = bf16[2048,128]{1,0:T(8,128)(2,1)S(1)} collective-permute-done((bf16[2048,128]{1,0:T(8,128)(2,1)S(1)}, bf16[2048,128]{1,0:T(8,128)(2,1)S(1)}, u32[]{:S(2)}, u32[]{:S(2)}) %collective-permute-start.13) | collective-permute-done | bytes 524320 | tf_op jit(solution)/shard_map/ppermute | solution.py:371
  74.5 2.6 %collective-permute-start.15 = (bf16[2048,128]{1,0:T(8,128)(2,1)S(1)}, bf16[2048,128]{1,0:T(8,128)(2,1)S(1)}, u32[]{:S(2)}, u32[]{:S(2)}) collective-permute-start(bf16[2048,128]{1,0:T(8,128)(2,1)S(1)} %get-tuple-element.52.own_ref), channel_id=1, source_target_pairs={{0,31},{1,2},{2,1},{3,4},{4,3},{5,6},{6,5},{7,8},{8,7},{9,10},{10,... | collective-permute-start | bytes 1572872 | tf_op jit(solution)/shard_map/ppermute | solution.py:371
  77.1 4.5 %shard_map.86.base_ref = f32[2048,128]{1,0:T(8,128)S(1)} custom-call(bf16[576,128,128]{2,1,0:T(8,128)(2,1)S(1)} %get-tuple-element.38.kept_ref, bf16[2048,128]{1,0:T(8,128)(2,1)S(1)} %get-tuple-element.52.own_ref, bf16[2048,128]{1,0:T(8,128)(2,1)S(1)} %collective-permute-done.16.near_ref, f32[2048,128]{1,0:T(8,128)S(1)} %get-tuple-element.53.x_ref, ...), custom_call_target="tpu_custom_call" | custom-call | flops 1744830464 | bytes 8000000 | tf_op jit(solution)/shard_map/pallas_call | solution.py:356
  81.5 4.9 %collective-permute-done.15.far_ref = bf16[2048,128]{1,0:T(8,128)(2,1)S(1)} collective-permute-done((bf16[2048,128]{1,0:T(8,128)(2,1)S(1)}, bf16[2048,128]{1,0:T(8,128)(2,1)S(1)}, u32[]{:S(2)}, u32[]{:S(2)}) %collective-permute-start.15) | collective-permute-done | bytes 524320 | tf_op jit(solution)/shard_map/ppermute | solution.py:371
  88.1 2.8 %collective-permute-start.17 = (bf16[2048,128]{1,0:T(8,128)(2,1)S(1)}, bf16[2048,128]{1,0:T(8,128)(2,1)S(1)}, u32[]{:S(2)}, u32[]{:S(2)}) collective-permute-start(bf16[2048,128]{1,0:T(8,128)(2,1)S(1)} %get-tuple-element.54.own_ref), channel_id=1, source_target_pairs={{0,31},{1,2},{2,1},{3,4},{4,3},{5,6},{6,5},{7,8},{8,7},{9,10},{10,... | collective-permute-start | bytes 1572872 | tf_op jit(solution)/shard_map/ppermute | solution.py:371
  90.9 4.5 %shard_map.88.base_ref = f32[2048,128]{1,0:T(8,128)S(1)} custom-call(bf16[576,128,128]{2,1,0:T(8,128)(2,1)S(1)} %get-tuple-element.38.kept_ref, bf16[2048,128]{1,0:T(8,128)(2,1)S(1)} %get-tuple-element.54.own_ref, bf16[2048,128]{1,0:T(8,128)(2,1)S(1)} %collective-permute-done.18.near_ref, f32[2048,128]{1,0:T(8,128)S(1)} %get-tuple-element.55.x_ref, ...), custom_call_target="tpu_custom_call" | custom-call | flops 1744830464 | bytes 8000000 | tf_op jit(solution)/shard_map/pallas_call | solution.py:356
  95.4 4.9 %collective-permute-done.17.far_ref = bf16[2048,128]{1,0:T(8,128)(2,1)S(1)} collective-permute-done((bf16[2048,128]{1,0:T(8,128)(2,1)S(1)}, bf16[2048,128]{1,0:T(8,128)(2,1)S(1)}, u32[]{:S(2)}, u32[]{:S(2)}) %collective-permute-start.17) | collective-permute-done | bytes 524320 | tf_op jit(solution)/shard_map/ppermute | solution.py:371
  102.0 2.6 %collective-permute-start.19 = (bf16[2048,128]{1,0:T(8,128)(2,1)S(1)}, bf16[2048,128]{1,0:T(8,128)(2,1)S(1)}, u32[]{:S(2)}, u32[]{:S(2)}) collective-permute-start(bf16[2048,128]{1,0:T(8,128)(2,1)S(1)} %get-tuple-element.56.own_ref), channel_id=1, source_target_pairs={{0,31},{1,2},{2,1},{3,4},{4,3},{5,6},{6,5},{7,8},{8,7},{9,10},{10,... | collective-permute-start | bytes 1572872 | tf_op jit(solution)/shard_map/ppermute | solution.py:371
  104.6 4.4 %shard_map.90.base_ref = f32[2048,128]{1,0:T(8,128)S(1)} custom-call(bf16[576,128,128]{2,1,0:T(8,128)(2,1)S(1)} %get-tuple-element.38.kept_ref, bf16[2048,128]{1,0:T(8,128)(2,1)S(1)} %get-tuple-element.56.own_ref, bf16[2048,128]{1,0:T(8,128)(2,1)S(1)} %collective-permute-done.20.near_ref, f32[2048,128]{1,0:T(8,128)S(1)} %get-tuple-element.57.x_ref, ...), custom_call_target="tpu_custom_call" | custom-call | flops 1744830464 | bytes 8000000 | tf_op jit(solution)/shard_map/pallas_call | solution.py:356
  109.0 5.0 %collective-permute-done.19.far_ref = bf16[2048,128]{1,0:T(8,128)(2,1)S(1)} collective-permute-done((bf16[2048,128]{1,0:T(8,128)(2,1)S(1)}, bf16[2048,128]{1,0:T(8,128)(2,1)S(1)}, u32[]{:S(2)}, u32[]{:S(2)}) %collective-permute-start.19) | collective-permute-done | bytes 524320 | tf_op jit(solution)/shard_map/ppermute | solution.py:371
  118.9 5.2 %collective-permute-done.22.far_ref = bf16[512,128]{1,0:T(8,128)(2,1)S(1)} collective-permute-done((bf16[512,128]{1,0:T(8,128)(2,1)S(1)}, bf16[512,128]{1,0:T(8,128)(2,1)S(1)}, u32[]{:S(2)}, u32[]{:S(2)}) %collective-permute-start.22) | collective-permute-done | bytes 131104 | tf_op jit(solution)/shard_map/ppermute | solution.py:371
  127.0 5.2 %collective-permute-done.24.far_ref = bf16[512,128]{1,0:T(8,128)(2,1)S(1)} collective-permute-done((bf16[512,128]{1,0:T(8,128)(2,1)S(1)}, bf16[512,128]{1,0:T(8,128)(2,1)S(1)}, u32[]{:S(2)}, u32[]{:S(2)}) %collective-permute-start.24) | collective-permute-done | bytes 131104 | tf_op jit(solution)/shard_map/ppermute | solution.py:371
  135.1 5.1 %shard_map.94.base_ref = f32[2048,128]{1,0:T(8,128)S(1)} custom-call(bf16[576,128,128]{2,1,0:T(8,128)(2,1)S(1)} %get-tuple-element.38.kept_ref, s32[16]{0:T(128)S(1)} %copy-done.2, bf16[512,128]{1,0:T(8,128)(2,1)S(1)} %shard_map.93.coarse_ref, bf16[512,128]{1,0:T(8,128)(2,1)S(1)} %collective-permute-done.26.near_ref, ...), custom_call_target="tpu_custom_call" | custom-call | flops 1744830464 | bytes 8000000 | tf_op jit(solution)/shard_map/pallas_call | solution.py:356
  142.1 2.8 %collective-permute-start.27 = (bf16[2048,128]{1,0:T(8,128)(2,1)S(1)}, bf16[2048,128]{1,0:T(8,128)(2,1)S(1)}, u32[]{:S(2)}, u32[]{:S(2)}) collective-permute-start(bf16[2048,128]{1,0:T(8,128)(2,1)S(1)} %get-tuple-element.63.own_ref), channel_id=1, source_target_pairs={{0,31},{1,2},{2,1},{3,4},{4,3},{5,6},{6,5},{7,8},{8,7},{9,10},{10,... | collective-permute-start | bytes 1572872 | tf_op jit(solution)/shard_map/ppermute | solution.py:371
  144.9 4.5 %shard_map.96.base_ref = f32[2048,128]{1,0:T(8,128)S(1)} custom-call(bf16[576,128,128]{2,1,0:T(8,128)(2,1)S(1)} %get-tuple-element.38.kept_ref, bf16[2048,128]{1,0:T(8,128)(2,1)S(1)} %get-tuple-element.63.own_ref, bf16[2048,128]{1,0:T(8,128)(2,1)S(1)} %collective-permute-done.28.near_ref, f32[2048,128]{1,0:T(8,128)S(1)} %get-tuple-element.64.x_ref, ...), custom_call_target="tpu_custom_call" | custom-call | flops 1744830464 | bytes 8000000 | tf_op jit(solution)/shard_map/pallas_call | solution.py:356
  149.4 5.0 %collective-permute-done.27.far_ref = bf16[2048,128]{1,0:T(8,128)(2,1)S(1)} collective-permute-done((bf16[2048,128]{1,0:T(8,128)(2,1)S(1)}, bf16[2048,128]{1,0:T(8,128)(2,1)S(1)}, u32[]{:S(2)}, u32[]{:S(2)}) %collective-permute-start.27) | collective-permute-done | bytes 524320 | tf_op jit(solution)/shard_map/ppermute | solution.py:371
  (69 shorter events, 43.7 us)
Async XLA Ops:
  1.7 6.5 %collective-permute-start = (bf16[2064,128]{1,0:T(8,128)(2,1)S(1)}, bf16[2064,128]{1,0:T(8,128)(2,1)S(1)}, u32[]{:S(2)}, u32[]{:S(2)}) collective-permute-start(bf16[2064,128]{1,0:T(8,128)(2,1)S(1)} %get-tuple-element.35.own_ref), channel_id=1, source_target_pairs={{0,1},{1,0},{2,3},{3,2},{4,5},{5,4},{6,7},{7,6},{8,9},{9,8},{10,11... | collective-permute-start | bytes 1585160 | tf_op jit(solution)/shard_map/ppermute | solution.py:374
  1.7 15.9 %collective-permute-start.4 = (bf16[2064,128]{1,0:T(8,128)(2,1)S(1)}, bf16[2064,128]{1,0:T(8,128)(2,1)S(1)}, u32[]{:S(2)}, u32[]{:S(2)}) collective-permute-start(bf16[2064,128]{1,0:T(8,128)(2,1)S(1)} %get-tuple-element.35.own_ref), channel_id=1, source_target_pairs={{0,31},{1,2},{2,1},{3,4},{4,3},{5,6},{6,5},{7,8},{8,7},{9,10},{10,... | collective-permute-start | bytes 1585160 | tf_op jit(solution)/shard_map/ppermute | solution.py:371
  19.2 7.5 %collective-permute-start.5 = (bf16[2048,128]{1,0:T(8,128)(2,1)S(1)}, bf16[2048,128]{1,0:T(8,128)(2,1)S(1)}, u32[]{:S(2)}, u32[]{:S(2)}) collective-permute-start(bf16[2048,128]{1,0:T(8,128)(2,1)S(1)} %get-tuple-element.40.own_ref), channel_id=1, source_target_pairs={{0,1},{1,0},{2,3},{3,2},{4,5},{5,4},{6,7},{7,6},{8,9},{9,8},{10,11... | collective-permute-start | bytes 1572872 | tf_op jit(solution)/shard_map/ppermute | solution.py:374
  19.3 13.2 %collective-permute-start.6 = (bf16[2048,128]{1,0:T(8,128)(2,1)S(1)}, bf16[2048,128]{1,0:T(8,128)(2,1)S(1)}, u32[]{:S(2)}, u32[]{:S(2)}) collective-permute-start(bf16[2048,128]{1,0:T(8,128)(2,1)S(1)} %get-tuple-element.40.own_ref), channel_id=1, source_target_pairs={{0,31},{1,2},{2,1},{3,4},{4,3},{5,6},{6,5},{7,8},{8,7},{9,10},{10,... | collective-permute-start | bytes 1572872 | tf_op jit(solution)/shard_map/ppermute | solution.py:371
  22.0 9.1 %collective-permute-start.3 = (bf16[400,128]{1,0:T(8,128)(2,1)S(1)}, bf16[400,128]{1,0:T(8,128)(2,1)S(1)}, u32[]{:S(2)}, u32[]{:S(2)}) collective-permute-start(bf16[400,128]{1,0:T(8,128)(2,1)S(1)} %shard_map.75.p0_ref), channel_id=1, source_target_pairs={{0,96},{32,0},{64,32},{96,64},{1,97},{33,1},{65,33},{97,65},{2,98}... | collective-permute-start | bytes 307208 | tf_op jit(solution)/shard_map/ppermute | solution.py:417
  25.1 6.2 %collective-permute-start.2 = (bf16[400,128]{1,0:T(8,128)(2,1)S(1)}, bf16[400,128]{1,0:T(8,128)(2,1)S(1)}, u32[]{:S(2)}, u32[]{:S(2)}) collective-permute-start(bf16[400,128]{1,0:T(8,128)(2,1)S(1)} %shard_map.75.p0_ref), channel_id=1, source_target_pairs={{0,64},{32,96},{64,0},{96,32},{1,65},{33,97},{65,1},{97,33},{2,66}... | collective-permute-start | bytes 307208 | tf_op jit(solution)/shard_map/ppermute | solution.py:417
  25.7 6.6 %collective-permute-start.1 = (bf16[400,128]{1,0:T(8,128)(2,1)S(1)}, bf16[400,128]{1,0:T(8,128)(2,1)S(1)}, u32[]{:S(2)}, u32[]{:S(2)}) collective-permute-start(bf16[400,128]{1,0:T(8,128)(2,1)S(1)} %shard_map.75.p0_ref), channel_id=1, source_target_pairs={{0,32},{32,64},{64,96},{96,0},{1,33},{33,65},{65,97},{97,1},{2,34}... | collective-permute-start | bytes 307208 | tf_op jit(solution)/shard_map/ppermute | solution.py:417
  34.8 7.8 %collective-permute-start.8 = (bf16[512,128]{1,0:T(8,128)(2,1)S(1)}, bf16[512,128]{1,0:T(8,128)(2,1)S(1)}, u32[]{:S(2)}, u32[]{:S(2)}) collective-permute-start(bf16[512,128]{1,0:T(8,128)(2,1)S(1)} %get-tuple-element.46.own_ref), channel_id=1, source_target_pairs={{0,31},{1,2},{2,1},{3,4},{4,3},{5,6},{6,5},{7,8},{8,7},{9,10},{10,... | collective-permute-start | bytes 393224 | tf_op jit(solution)/shard_map/ppermute | solution.py:371
  36.8 5.8 %collective-permute-start.7 = (bf16[512,128]{1,0:T(8,128)(2,1)S(1)}, bf16[512,128]{1,0:T(8,128)(2,1)S(1)}, u32[]{:S(2)}, u32[]{:S(2)}) collective-permute-start(bf16[512,128]{1,0:T(8,128)(2,1)S(1)} %get-tuple-element.46.own_ref), channel_id=1, source_target_pairs={{0,1},{1,0},{2,3},{3,2},{4,5},{5,4},{6,7},{7,6},{8,9},{9,8},{10,11... | collective-permute-start | bytes 393224 | tf_op jit(solution)/shard_map/ppermute | solution.py:374
  42.9 7.8 %collective-permute-start.10 = (bf16[512,128]{1,0:T(8,128)(2,1)S(1)}, bf16[512,128]{1,0:T(8,128)(2,1)S(1)}, u32[]{:S(2)}, u32[]{:S(2)}) collective-permute-start(bf16[512,128]{1,0:T(8,128)(2,1)S(1)} %get-tuple-element.48.own_ref), channel_id=1, source_target_pairs={{0,31},{1,2},{2,1},{3,4},{4,3},{5,6},{6,5},{7,8},{8,7},{9,10},{10,... | collective-permute-start | bytes 393224 | tf_op jit(solution)/shard_map/ppermute | solution.py:371
  44.9 5.8 %collective-permute-start.9 = (bf16[512,128]{1,0:T(8,128)(2,1)S(1)}, bf16[512,128]{1,0:T(8,128)(2,1)S(1)}, u32[]{:S(2)}, u32[]{:S(2)}) collective-permute-start(bf16[512,128]{1,0:T(8,128)(2,1)S(1)} %get-tuple-element.48.own_ref), channel_id=1, source_target_pairs={{0,1},{1,0},{2,3},{3,2},{4,5},{5,4},{6,7},{7,6},{8,9},{9,8},{10,11... | collective-permute-start | bytes 393224 | tf_op jit(solution)/shard_map/ppermute | solution.py:374
  51.1 8.0 %collective-permute-start.11 = (bf16[512,128]{1,0:T(8,128)(2,1)S(1)}, bf16[512,128]{1,0:T(8,128)(2,1)S(1)}, u32[]{:S(2)}, u32[]{:S(2)}) collective-permute-start(bf16[512,128]{1,0:T(8,128)(2,1)S(1)} %shard_map.81.coarse_ref), channel_id=1, source_target_pairs={{0,31},{1,2},{2,1},{3,4},{4,3},{5,6},{6,5},{7,8},{8,7},{9,10},{10,... | collective-permute-start | bytes 393224 | tf_op jit(solution)/shard_map/ppermute | solution.py:371
  60.8 12.0 %collective-permute-start.13 = (bf16[2048,128]{1,0:T(8,128)(2,1)S(1)}, bf16[2048,128]{1,0:T(8,128)(2,1)S(1)}, u32[]{:S(2)}, u32[]{:S(2)}) collective-permute-start(bf16[2048,128]{1,0:T(8,128)(2,1)S(1)} %get-tuple-element.50.own_ref), channel_id=1, source_target_pairs={{0,31},{1,2},{2,1},{3,4},{4,3},{5,6},{6,5},{7,8},{8,7},{9,10},{10,... | collective-permute-start | bytes 1572872 | tf_op jit(solution)/shard_map/ppermute | solution.py:371
  74.5 12.0 %collective-permute-start.15 = (bf16[2048,128]{1,0:T(8,128)(2,1)S(1)}, bf16[2048,128]{1,0:T(8,128)(2,1)S(1)}, u32[]{:S(2)}, u32[]{:S(2)}) collective-permute-start(bf16[2048,128]{1,0:T(8,128)(2,1)S(1)} %get-tuple-element.52.own_ref), channel_id=1, source_target_pairs={{0,31},{1,2},{2,1},{3,4},{4,3},{5,6},{6,5},{7,8},{8,7},{9,10},{10,... | collective-permute-start | bytes 1572872 | tf_op jit(solution)/shard_map/ppermute | solution.py:371
  88.0 2.9 %collective-permute-start.18 = (bf16[2048,128]{1,0:T(8,128)(2,1)S(1)}, bf16[2048,128]{1,0:T(8,128)(2,1)S(1)}, u32[]{:S(2)}, u32[]{:S(2)}) collective-permute-start(bf16[2048,128]{1,0:T(8,128)(2,1)S(1)} %get-tuple-element.54.own_ref), channel_id=1, source_target_pairs={{0,1},{1,0},{2,3},{3,2},{4,5},{5,4},{6,7},{7,6},{8,9},{9,8},{10,11... | collective-permute-start | bytes 1572872 | tf_op jit(solution)/shard_map/ppermute | solution.py:374
  88.1 12.2 %collective-permute-start.17 = (bf16[2048,128]{1,0:T(8,128)(2,1)S(1)}, bf16[2048,128]{1,0:T(8,128)(2,1)S(1)}, u32[]{:S(2)}, u32[]{:S(2)}) collective-permute-start(bf16[2048,128]{1,0:T(8,128)(2,1)S(1)} %get-tuple-element.54.own_ref), channel_id=1, source_target_pairs={{0,31},{1,2},{2,1},{3,4},{4,3},{5,6},{6,5},{7,8},{8,7},{9,10},{10,... | collective-permute-start | bytes 1572872 | tf_op jit(solution)/shard_map/ppermute | solution.py:371
  102.0 12.0 %collective-permute-start.19 = (bf16[2048,128]{1,0:T(8,128)(2,1)S(1)}, bf16[2048,128]{1,0:T(8,128)(2,1)S(1)}, u32[]{:S(2)}, u32[]{:S(2)}) collective-permute-start(bf16[2048,128]{1,0:T(8,128)(2,1)S(1)} %get-tuple-element.56.own_ref), channel_id=1, source_target_pairs={{0,31},{1,2},{2,1},{3,4},{4,3},{5,6},{6,5},{7,8},{8,7},{9,10},{10,... | collective-permute-start | bytes 1572872 | tf_op jit(solution)/shard_map/ppermute | solution.py:371
  116.3 7.8 %collective-permute-start.22 = (bf16[512,128]{1,0:T(8,128)(2,1)S(1)}, bf16[512,128]{1,0:T(8,128)(2,1)S(1)}, u32[]{:S(2)}, u32[]{:S(2)}) collective-permute-start(bf16[512,128]{1,0:T(8,128)(2,1)S(1)} %get-tuple-element.59.own_ref), channel_id=1, source_target_pairs={{0,31},{1,2},{2,1},{3,4},{4,3},{5,6},{6,5},{7,8},{8,7},{9,10},{10,... | collective-permute-start | bytes 393224 | tf_op jit(solution)/shard_map/ppermute | solution.py:371
  118.9 5.2 %collective-permute-start.21 = (bf16[512,128]{1,0:T(8,128)(2,1)S(1)}, bf16[512,128]{1,0:T(8,128)(2,1)S(1)}, u32[]{:S(2)}, u32[]{:S(2)}) collective-permute-start(bf16[512,128]{1,0:T(8,128)(2,1)S(1)} %get-tuple-element.59.own_ref), channel_id=1, source_target_pairs={{0,1},{1,0},{2,3},{3,2},{4,5},{5,4},{6,7},{7,6},{8,9},{9,8},{10,11... | collective-permute-start | bytes 393224 | tf_op jit(solution)/shard_map/ppermute | solution.py:374
  124.3 7.8 %collective-permute-start.24 = (bf16[512,128]{1,0:T(8,128)(2,1)S(1)}, bf16[512,128]{1,0:T(8,128)(2,1)S(1)}, u32[]{:S(2)}, u32[]{:S(2)}) collective-permute-start(bf16[512,128]{1,0:T(8,128)(2,1)S(1)} %get-tuple-element.61.own_ref), channel_id=1, source_target_pairs={{0,31},{1,2},{2,1},{3,4},{4,3},{5,6},{6,5},{7,8},{8,7},{9,10},{10,... | collective-permute-start | bytes 393224 | tf_op jit(solution)/shard_map/ppermute | solution.py:371
  127.0 5.2 %collective-permute-start.23 = (bf16[512,128]{1,0:T(8,128)(2,1)S(1)}, bf16[512,128]{1,0:T(8,128)(2,1)S(1)}, u32[]{:S(2)}, u32[]{:S(2)}) collective-permute-start(bf16[512,128]{1,0:T(8,128)(2,1)S(1)} %get-tuple-element.61.own_ref), channel_id=1, source_target_pairs={{0,1},{1,0},{2,3},{3,2},{4,5},{5,4},{6,7},{7,6},{8,9},{9,8},{10,11... | collective-permute-start | bytes 393224 | tf_op jit(solution)/shard_map/ppermute | solution.py:374
  132.5 7.8 %collective-permute-start.25 = (bf16[512,128]{1,0:T(8,128)(2,1)S(1)}, bf16[512,128]{1,0:T(8,128)(2,1)S(1)}, u32[]{:S(2)}, u32[]{:S(2)}) collective-permute-start(bf16[512,128]{1,0:T(8,128)(2,1)S(1)} %shard_map.93.coarse_ref), channel_id=1, source_target_pairs={{0,31},{1,2},{2,1},{3,4},{4,3},{5,6},{6,5},{7,8},{8,7},{9,10},{10,... | collective-permute-start | bytes 393224 | tf_op jit(solution)/shard_map/ppermute | solution.py:371
  142.0 2.9 %collective-permute-start.28 = (bf16[2048,128]{1,0:T(8,128)(2,1)S(1)}, bf16[2048,128]{1,0:T(8,128)(2,1)S(1)}, u32[]{:S(2)}, u32[]{:S(2)}) collective-permute-start(bf16[2048,128]{1,0:T(8,128)(2,1)S(1)} %get-tuple-element.63.own_ref), channel_id=1, source_target_pairs={{0,1},{1,0},{2,3},{3,2},{4,5},{5,4},{6,7},{7,6},{8,9},{9,8},{10,11... | collective-permute-start | bytes 1572872 | tf_op jit(solution)/shard_map/ppermute | solution.py:374
  142.1 12.3 %collective-permute-start.27 = (bf16[2048,128]{1,0:T(8,128)(2,1)S(1)}, bf16[2048,128]{1,0:T(8,128)(2,1)S(1)}, u32[]{:S(2)}, u32[]{:S(2)}) collective-permute-start(bf16[2048,128]{1,0:T(8,128)(2,1)S(1)} %get-tuple-element.63.own_ref), channel_id=1, source_target_pairs={{0,31},{1,2},{2,1},{3,4},{4,3},{5,6},{6,5},{7,8},{8,7},{9,10},{10,... | collective-permute-start | bytes 1572872 | tf_op jit(solution)/shard_map/ppermute | solution.py:371
  (10 other events, 72.5 us)
where the time goes:
time: 157 us
  Pallas kernels  65.1 us (41%)
  waiting for transfers between devices  48.6 us (31%)
  starting transfers between devices  42 us (27%)
    pallas_call x25, Pallas kernels, run(): pl.pallas_call(kernel, out_shape=[jax.ShapeDtypeStruct(shape, dtype) if t...  65.1 us
    ppermute x13, waiting for transfers between devices, swap(): lax.ppermute(x, 'rows', [(i, (i - 1) % size if i % 2 == 0 else (i + 1) %...  47.3 us
    ppermute x13, starting transfers between devices, swap(): lax.ppermute(x, 'rows', [(i, (i - 1) % size if i % 2 == 0 else (i + 1) %...  36.5 us
    ppermute x3, starting transfers between devices, shards(): lax.ppermute(packed, 'rhs', [(i, (i + k) % 4) for i in range(4)])  4.68 us
  transfers between devices with their start and end apart: 29, of which 12 were waited for; matrix products, arithmetic and copies ran while one was open for 0% of the time, Pallas kernels for 29%

commit v1 on v0

v1 whole, which is shorter than its diff:
```python
import functools

import jax
import jax.numpy as jnp
from jax import lax
from jax.experimental import pallas as pl
from jax.experimental.pallas import tpu as pltpu
from jax.sharding import PartitionSpec as P

CYCLES = 2
CHEB = 3
RELAX = 0.7
THETA = 1.0
DELTA = 0.6

B = 128
ROWS = 16
GROUP = 4
TILE = GROUP * B
TILE_ROWS = ROWS // GROUP
SLOTS = 36
FIELD = ROWS * B
TAIL = 16
QROWS = 4 * B
PIECE = 3 * TILE

f32 = jnp.float32
bf16 = jnp.bfloat16
VMEM_SPEC = pl.BlockSpec(memory_space=pltpu.VMEM)
SMEM_SPEC = pl.BlockSpec(memory_space=pltpu.SMEM)
ANY_SPEC = pl.BlockSpec(memory_space=pl.ANY)
LIMIT = 12 * 1024 * 1024


def resident(x):
    return pltpu.with_memory_space_constraint(x, pltpu.VMEM)


def core_of():
    return lax.rem(lax.axis_index("rows"), 2)


def column(row):
    return jnp.transpose(jnp.broadcast_to(row, (B, B)))


def places(columns_ref, out_ref):
    row = lax.broadcasted_iota(jnp.int32, (ROWS, 2 * ROWS), 0)
    first = lax.axis_index("rows") * ROWS - ROWS
    offset = jnp.bitwise_and(columns_ref[...] - first - row + 512, 511)
    offset = jnp.minimum(offset, 2 * ROWS)
    start = row * SLOTS + jnp.bitwise_and(row, GROUP - 1)
    missing = ROWS * (2 * ROWS + 1) - jnp.sum(offset, axis=1, keepdims=True)
    missing = jnp.clip(missing, 0, 2 * ROWS) + start[:, 0:1]
    out_ref[:, 0 : 2 * ROWS] = start + offset
    out_ref[:, 2 * ROWS : B] = jnp.broadcast_to(missing, (ROWS, B - 2 * ROWS))


def start_kernel(
    right_ref, diag_ref, group_ref, coarse_ref, coarse_diag_ref, columns_ref,
    first_ref, sent_ref, head_ref, rest_ref, ratio_ref, diag_out_ref, packed_ref, places_ref,
    right_s, diag_s, group_s, coarse_s, coarse_diag_s, columns_s, sems,
):
    chunks = [
        pltpu.make_async_copy(
            right_ref.at[pl.ds(g * TILE, TILE), :], right_s.at[pl.ds(g * TILE, TILE), :], sems.at[g]
        )
        for g in range(TILE_ROWS)
    ]
    diag_copy = pltpu.make_async_copy(diag_ref, diag_s, sems.at[TILE_ROWS])
    group_copy = pltpu.make_async_copy(group_ref, group_s, sems.at[TILE_ROWS + 1])
    coarse_copy = pltpu.make_async_copy(coarse_ref, coarse_s, sems.at[TILE_ROWS + 2])
    coarse_diag_copy = pltpu.make_async_copy(coarse_diag_ref, coarse_diag_s, sems.at[TILE_ROWS + 3])
    columns_copy = pltpu.make_async_copy(columns_ref, columns_s, sems.at[TILE_ROWS + 4])
    columns_copy.start()
    coarse_diag_copy.start()
    coarse_copy.start()
    diag_copy.start()
    for chunk in chunks:
        chunk.start()
    group_copy.start()
    columns_copy.wait()
    places(columns_s, places_ref)
    coarse_diag_copy.wait()
    coarse_copy.wait()
    pack(coarse_s, coarse_diag_s, packed_ref)
    diag_copy.wait()
    for g in range(TILE_ROWS):
        chunks[g].wait()
        for r in range(g * GROUP, (g + 1) * GROUP):
            rows = pl.ds(r * B, B)
            diag = column(diag_s[r : r + 1, :])
            ratio = RELAX / diag
            value = ratio * right_s[rows, :]
            diag_out_ref[rows, :] = diag
            ratio_ref[rows, :] = ratio
            first_ref[rows, :] = value
            sent_ref[rows, :] = value.astype(bf16)
    even = core_of() == 0
    head = pl.multiple_of(jnp.where(even, 0, TILE), TILE)
    rest = pl.multiple_of(jnp.where(even, PIECE, 0), TILE)
    head_ref[pl.ds(0, PIECE), :] = sent_ref[pl.ds(head, PIECE), :]
    rest_ref[...] = sent_ref[pl.ds(rest, TILE), :]
    group_copy.wait()
    size = lax.axis_size("rows")
    index = lax.broadcasted_iota(jnp.int32, (TAIL, B), 0)
    tail = jnp.zeros((TAIL, B), f32)
    for r in range(ROWS):
        tail = jnp.where(index == r, lax.div(group_s[r], size).astype(f32), tail)
    sent_ref[pl.ds(FIELD, TAIL), :] = tail.astype(bf16)
    head_ref[pl.ds(PIECE, TAIL), :] = tail.astype(bf16)


def pack(blocks_ref, diag_ref, out_ref):
    inverse = 1.0 / diag_ref[...]
    scale = column(inverse)
    for d in range(3):
        out_ref[pl.ds(d * B, B), :] = (scale * blocks_ref[0, d]).astype(bf16)
    high = inverse.astype(bf16).astype(f32)
    low = inverse - high
    index = lax.broadcasted_iota(jnp.int32, (TAIL, B), 0)
    out_ref[pl.ds(3 * B, TAIL), :] = jnp.where(index == 0, high, low).astype(bf16)


def sort_kernel(p0_ref, p1_ref, p2_ref, p3_ref, after_ref, ops_ref, scale_ref):
    me = lax.axis_index("rhs")
    for k, ref in enumerate((p0_ref, p1_ref, p2_ref, p3_ref)):
        q = jnp.bitwise_and(me - k + 4, 3)
        for d in range(3):
            ops_ref[q * 3 + d] = ref[pl.ds(d * B, B), :]
        tail = ref[pl.ds(3 * B, TAIL), :].astype(f32)
        scale_ref[pl.ds(q * B, B), :] = column(tail[0:1, :] + tail[1:2, :])


def tile_product(kept_ref, group, slot, count, field):
    lhs = jnp.concatenate(
        [
            jnp.concatenate(
                [kept_ref[(group * GROUP + a) * SLOTS + slot + b] for b in range(GROUP * count)],
                axis=1,
            )
            for a in range(GROUP)
        ],
        axis=0,
    )
    return jnp.dot(lhs, field, preferred_element_type=f32)


def rows_of(group):
    return pl.ds(pl.multiple_of(group * TILE, TILE), TILE)


def field_at(ref, tile, count):
    return ref[pl.ds(pl.multiple_of(tile * TILE, TILE), count * TILE), :]


def group_of(upper, m):
    return jnp.where(upper, m, TILE_ROWS - 1 - m)


def side_slot(upper, m, j):
    return jnp.where(upper, GROUP * (2 * TILE_ROWS - m + j), GROUP * j)


def near_products(kept_ref, own_ref, near_ref, first, second, straight=False, ready=None):
    @pl.loop(0, TILE_ROWS)
    def _(group):
        if ready is not None:
            ready(group)
        part = tile_product(
            kept_ref, group, GROUP * (TILE_ROWS - group), TILE_ROWS, own_ref[pl.ds(0, FIELD), :]
        )
        first(rows_of(group), part)

    upper = core_of() == 0

    def side(m, j, count):
        group = group_of(upper, m)
        field = field_at(near_ref, jnp.where(upper, j, TILE_ROWS - 1 - m + j), count)
        second(rows_of(group), tile_product(kept_ref, group, side_slot(upper, m, j), count, field))

    if straight:
        for m in range(TILE_ROWS):
            side(m, 0, m + 1)
        return

    @pl.loop(0, 4)
    def _(p):
        side(jnp.minimum(p + 1, 3), jnp.where(p == 3, 2, 0), 2)

    @pl.loop(0, 2)
    def _(p):
        side(2 * p, 2 * p, 1)


def far_products(kept_ref, far_ref, emit):
    upper = core_of() == 1
    for m in range(TILE_ROWS):
        group = group_of(upper, m)
        field = field_at(far_ref, jnp.where(upper, 0, TILE_ROWS - 1 - m), m + 1)
        emit(m, rows_of(group), tile_product(kept_ref, group, side_slot(upper, m, 0), m + 1, field))


def head_products(kept_ref, head_ref, emit):
    upper = core_of() == 1
    for m in range(TILE_ROWS - 1):
        group = group_of(upper, m)
        field = field_at(head_ref, jnp.where(upper, 0, TILE_ROWS - 2 - m), m + 1)
        emit(m, rows_of(group), tile_product(kept_ref, group, side_slot(upper, m, 0), m + 1, field))
    m = TILE_ROWS - 1
    group = group_of(upper, m)
    slot = jnp.where(upper, side_slot(True, m, 0), side_slot(False, m, 1))
    emit(m, rows_of(group), tile_product(kept_ref, group, slot, m, field_at(head_ref, 0, m)))


def rest_product(kept_ref, rest_ref):
    upper = core_of() == 1
    m = TILE_ROWS - 1
    group = group_of(upper, m)
    slot = jnp.where(upper, side_slot(True, m, m), side_slot(False, m, 0))
    return rows_of(group), tile_product(kept_ref, group, slot, 1, rest_ref[...])


def send(m, rows, value, sent_ref, head_ref, rest_ref):
    value = value.astype(bf16)
    sent_ref[rows, :] = value
    if m == 0:
        rest_ref[...] = value
    else:
        at = jnp.where(core_of() == 1, m - 1, TILE_ROWS - 1 - m)
        head_ref[rows_of(at), :] = value


def sweep_near(
    kept_ref, own_ref, near_ref, x_ref, first_ref, ratio_ref, base_ref, straight=False, ready=None
):
    def first(rows, part):
        base_ref[rows, :] = (1.0 - RELAX) * x_ref[rows, :] + first_ref[rows, :] - ratio_ref[rows, :] * part

    def second(rows, part):
        base_ref[rows, :] -= ratio_ref[rows, :] * part

    near_products(kept_ref, own_ref, near_ref, first, second, straight, ready)


def sweep_near_kernel(kept_ref, own_ref, near_ref, x_ref, first_ref, ratio_ref, base_ref):
    sweep_near(kept_ref, own_ref, near_ref, x_ref, first_ref, ratio_ref, base_ref)


def load_near_kernel(
    places_ref, blocks_ref, own_ref, near_ref, first_ref, ratio_ref, kept_ref, base_ref, sems
):
    empty = jnp.zeros((B, B), bf16)

    @pl.loop(0, ROWS)
    def _(r):
        sem = sems.at[lax.div(r, GROUP)]
        for k in range(2 * ROWS):
            pltpu.make_async_copy(blocks_ref.at[r, k], kept_ref.at[places_ref[r, k]], sem).start()

    for r in range(ROWS):
        lead = r % GROUP
        kept_ref[places_ref[r, 2 * ROWS]] = empty
        for pad in range(GROUP - 1):
            kept_ref[r * SLOTS + (pad if pad < lead else 2 * ROWS + 1 + pad)] = empty

    def ready(group):
        for a in range(GROUP):
            r = group * GROUP + a
            pltpu.make_async_copy(
                blocks_ref.at[r], kept_ref.at[pl.ds(r * 2 * ROWS, 2 * ROWS)], sems.at[group]
            ).wait()

    sweep_near(
        kept_ref, own_ref, near_ref, first_ref, first_ref, ratio_ref, base_ref, True, ready
    )


def sweep_head_kernel(kept_ref, far_ref, base_ref, ratio_ref, x_ref, sent_ref, head_ref, rest_ref):
    def emit(m, rows, part):
        value = base_ref[rows, :] - ratio_ref[rows, :] * part
        x_ref[rows, :] = value
        if m < TILE_ROWS - 1:
            send(m, rows, value, sent_ref, head_ref, rest_ref)

    head_products(kept_ref, far_ref, emit)


def sweep_rest_kernel(
    kept_ref, far_ref, ratio_ref, x_in, sent_in, head_in, x_ref, sent_ref, head_ref
):
    rows, part = rest_product(kept_ref, far_ref)
    value = x_in[rows, :] - ratio_ref[rows, :] * part
    x_ref[rows, :] = value
    send(TILE_ROWS - 1, rows, value, sent_ref, head_ref, None)


def last_head_kernel(kept_ref, far_ref, base_ref, ratio_ref, x_ref):
    def emit(m, rows, part):
        x_ref[rows, :] = base_ref[rows, :] - ratio_ref[rows, :] * part

    head_products(kept_ref, far_ref, emit)


def last_rest_kernel(kept_ref, far_ref, ratio_ref, x_in, x_ref, x_s, sems):
    upper = core_of() == 1
    copies = []
    for m in range(TILE_ROWS - 1):
        done = rows_of(group_of(upper, m))
        copies.append(pltpu.make_async_copy(x_in.at[done, :], x_ref.at[done, :], sems.at[m]))
        copies[m].start()
    rows, part = rest_product(kept_ref, far_ref)
    x_s[...] = x_in[rows, :] - ratio_ref[rows, :] * part
    copies.append(pltpu.make_async_copy(x_s, x_ref.at[rows, :], sems.at[TILE_ROWS - 1]))
    copies[-1].start()
    for copy in copies:
        copy.wait()


def residual_near_kernel(
    straight, kept_ref, own_ref, near_ref, x_ref, right_ref, diag_ref, base_ref
):
    def first(rows, part):
        base_ref[rows, :] = right_ref[rows, :] - diag_ref[rows, :] * x_ref[rows, :] - part

    def second(rows, part):
        base_ref[rows, :] -= part

    near_products(kept_ref, own_ref, near_ref, first, second, straight)


def residual_head_kernel(kept_ref, group_ref, far_ref, base_ref, res_ref, side_ref):
    side_ref[...] = jnp.zeros((QROWS, B), f32)
    upper = core_of() == 1

    def emit(m, rows, part):
        value = base_ref[rows, :] - part
        res_ref[rows, :] = value
        if m < TILE_ROWS - 1:
            for a in range(GROUP):
                group = lax.div(group_ref[group_of(upper, m) * GROUP + a], lax.axis_size("rows"))
                side_ref[pl.ds(pl.multiple_of(group * B, B), B), :] += value[a * B : (a + 1) * B, :]

    head_products(kept_ref, far_ref, emit)


def residual_far_kernel(
    kept_ref, group_ref, far_ref, base_ref, scale_ref, res_ref, side_ref, sent_ref
):
    upper = core_of() == 1
    side_ref[...] = jnp.zeros((QROWS, B), f32)

    def emit(m, rows, part):
        value = base_ref[rows, :] - part
        res_ref[rows, :] = value
        for a in range(GROUP):
            group = lax.div(group_ref[group_of(upper, m) * GROUP + a], lax.axis_size("rows"))
            side_ref[pl.ds(pl.multiple_of(group * B, B), B), :] += value[a * B : (a + 1) * B, :]

    far_products(kept_ref, far_ref, emit)
    value = scale_ref[...] * side_ref[...]
    side_ref[...] = value
    sent_ref[...] = value.astype(bf16)


def residual_rest_kernel(
    kept_ref, tail_ref, far_ref, scale_ref, res_in, side_in, res_ref, side_ref, sent_ref
):
    upper = (core_of() == 1).astype(f32)
    tail = tail_ref[pl.ds(FIELD, TAIL), :].astype(f32)
    rows, part = rest_product(kept_ref, far_ref)
    value = res_in[rows, :] - part
    res_ref[rows, :] = value
    for q in range(4):
        place = pl.ds(q * B, B)
        total = side_in[place, :]
        for a in range(GROUP):
            at = TAIL - GROUP + a
            group = upper * tail[at : at + 1, :] + (1.0 - upper) * tail[a : a + 1, :]
            total = total + jnp.where(group == q, 1.0, 0.0) * value[a * B : (a + 1) * B, :]
        total = scale_ref[place, :] * total
        side_ref[place, :] = total
        sent_ref[place, :] = total.astype(bf16)


def spread(coarse_ref, tail_ref, start, out_ref):
    tail = tail_ref[pl.ds(start, TAIL), :].astype(f32)
    parts = [coarse_ref[pl.ds(q * B, B), :].astype(f32) for q in range(4)]
    for r in range(ROWS):
        group = tail[r : r + 1, :]
        value = jnp.where(group < 0.5, parts[0], parts[1])
        value = jnp.where(group < 1.5, value, parts[2])
        value = jnp.where(group < 2.5, value, parts[3])
        out_ref[pl.ds(r * B, B), :] = value.astype(bf16)


def lift_near_kernel(
    kept_ref, group_ref, coarse_ref, near_ref, near_tail_ref, x_ref, res_ref, ratio_ref, base_ref, own_s, near_s
):
    for r in range(ROWS):
        rows = pl.ds(pl.multiple_of(lax.div(group_ref[r], lax.axis_size("rows")) * B, B), B)
        own_s[pl.ds(r * B, B), :] = coarse_ref[rows, :]
    spread(near_ref, near_tail_ref, FIELD, near_s)

    def first(rows, part):
        base_ref[rows, :] = (
            x_ref[rows, :]
            + (1.0 - RELAX) * own_s[rows, :].astype(f32)
            + ratio_ref[rows, :] * (res_ref[rows, :] - part)
        )

    def second(rows, part):
        base_ref[rows, :] -= ratio_ref[rows, :] * part

    near_products(kept_ref, own_s, near_s, first, second)


def lift_far_kernel(
    kept_ref, far_ref, far_tail_ref, base_ref, ratio_ref, x_ref, sent_ref, head_ref, rest_ref, far_s
):
    spread(far_ref, far_tail_ref, PIECE, far_s)

    def emit(m, rows, part):
        value = base_ref[rows, :] - ratio_ref[rows, :] * part
        x_ref[rows, :] = value
        send(m, rows, value, sent_ref, head_ref, rest_ref)

    far_products(kept_ref, far_s, emit)


def coarse_terms(ops_ref, own_ref, near_ref, far_ref, emit):
    i = lax.axis_index("rows")
    last = lax.axis_size("rows") - 1
    near_is_upper = (core_of() == 0).astype(f32)
    step_up = (i == last).astype(jnp.int32)
    step_down = (i == 0).astype(jnp.int32)
    for q in range(4):
        at_up = pl.multiple_of(jnp.minimum(q + step_up, 3) * B, B)
        at_down = pl.multiple_of(jnp.maximum(q - step_down, 0) * B, B)
        keep_up = (q + step_up <= 3).astype(f32)
        keep_down = (q - step_down >= 0).astype(f32)
        upper = near_is_upper * near_ref[pl.ds(at_up, B), :].astype(f32) + (
            1.0 - near_is_upper
        ) * far_ref[pl.ds(at_up, B), :].astype(f32)
        lower = near_is_upper * far_ref[pl.ds(at_down, B), :].astype(f32) + (
            1.0 - near_is_upper
        ) * near_ref[pl.ds(at_down, B), :].astype(f32)
        field = jnp.concatenate(
            [
                (keep_down * lower).astype(bf16),
                own_ref[pl.ds(q * B, B), :],
                (keep_up * upper).astype(bf16),
            ],
            axis=0,
        )
        ops = jnp.concatenate([ops_ref[q * 3 + d] for d in range(3)], axis=1)
        emit(pl.ds(q * B, B), jnp.dot(ops, field, preferred_element_type=f32))


def ratios():
    sigma = THETA / DELTA
    old = 1.0 / sigma
    out = []
    for _ in range(CHEB - 1):
        new = 1.0 / (2.0 * sigma - old)
        out.append((new * old, 2.0 * new / DELTA))
        old = new
    return out


def coarse_first_kernel(ops_ref, side_ref, own_ref, near_ref, far_ref, fix_ref, sent_ref):
    keep, gain = ratios()[0]

    def emit(rows, part):
        side = side_ref[rows, :] / THETA
        fix = side + keep * side + gain * (side_ref[rows, :] - side - part)
        fix_ref[rows, :] = fix
        sent_ref[rows, :] = fix.astype(bf16)

    coarse_terms(ops_ref, own_ref, near_ref, far_ref, emit)


def coarse_second_kernel(ops_ref, side_ref, fix_ref, own_ref, near_ref, far_ref, sent_ref):
    keep, gain = ratios()[1]

    def emit(rows, part):
        fix = fix_ref[rows, :]
        update = fix - side_ref[rows, :] / THETA
        fix = fix + keep * update + gain * (side_ref[rows, :] - fix - part)
        sent_ref[rows, :] = fix.astype(bf16)

    coarse_terms(ops_ref, own_ref, near_ref, far_ref, emit)


def run(kernel, outs, args, scratch=(), cost=(0, 0), hbm_outs=(), alias={}):
    specs, values = [], []
    for value, space in args:
        if space == "v":
            specs.append(VMEM_SPEC)
            values.append(resident(value))
        elif space == "b":
            specs.append(VMEM_SPEC)
            values.append(value)
        elif space == "s":
            specs.append(SMEM_SPEC)
            values.append(value)
        elif space == "a":
            specs.append(ANY_SPEC)
            values.append(value)
        else:
            specs.append(ANY_SPEC)
            values.append(pltpu.with_memory_space_constraint(value, pltpu.HBM))
    return pl.pallas_call(
        kernel,
        out_shape=[
            jax.ShapeDtypeStruct(shape, dtype) if n in hbm_outs else pltpu.VMEM(shape, dtype)
            for n, (shape, dtype) in enumerate(outs)
        ],
        in_specs=specs,
        out_specs=[ANY_SPEC if n in hbm_outs else VMEM_SPEC for n in range(len(outs))],
        input_output_aliases=alias,
        scratch_shapes=list(scratch),
        cost_estimate=pl.CostEstimate(flops=cost[0], bytes_accessed=cost[1], transcendentals=0),
        compiler_params=pltpu.CompilerParams(vmem_limit_bytes=LIMIT),
    )(*values)


def swap_near(x, size):
    return lax.ppermute(x, "rows", [(i, i ^ 1) for i in range(size)])


def swap_far(x, size):
    pairs = [(i, (i - 1) % size if i % 2 == 0 else (i + 1) % size) for i in range(size)]
    return lax.ppermute(x, "rows", pairs)


FULL = (FIELD, B)
HEAD = (PIECE, B)
REST = (TILE, B)
SIDE = (QROWS, B)
TILE_FLOPS = 2 * TILE * TILE * B
NEAR_COST = (26 * TILE_FLOPS, 8_000_000)
HEAD_COST = (9 * TILE_FLOPS, 3_000_000)
REST_COST = (TILE_FLOPS, 1_000_000)
FIELDS = [(FULL, f32), (FULL, bf16), (HEAD, bf16), (REST, bf16)]


def shards(right_side, fine_blocks, fine_columns, fine_diag, aggregate, coarse_blocks, coarse_diag):
    size = lax.axis_size("rows")

    first, sent, head, rest, ratio, diag, packed, places_of = run(
        start_kernel,
        [
            (FULL, f32), ((FIELD + TAIL, B), bf16), ((PIECE + TAIL, B), bf16), (REST, bf16),
            (FULL, f32), (FULL, f32), ((3 * B + TAIL, B), bf16),
            ((ROWS, B), jnp.int32),
        ],
        [
            (right_side, "h"), (fine_diag.reshape(ROWS, B), "h"), (aggregate, "h"),
            (coarse_blocks, "h"), (coarse_diag.reshape(1, B), "h"),
            (fine_columns, "h"),
        ],
        [
            pltpu.VMEM(FULL, f32),
            pltpu.VMEM((ROWS, B), f32),
            pltpu.SMEM((ROWS,), jnp.int32),
            pltpu.VMEM((1, 3, B, B), f32),
            pltpu.VMEM((1, B), f32),
            pltpu.VMEM((ROWS, 2 * ROWS), jnp.int32),
            pltpu.SemaphoreType.DMA((TILE_ROWS + 5,)),
        ],
    )

    def swap_fields(sent, head, rest):
        return swap_far(head, size), swap_far(rest, size), swap_near(sent, size)

    def swap_sides(sent):
        return swap_far(sent, size), swap_near(sent, size)

    pieces = [packed] + [
        lax.ppermute(packed, "rhs", [(i, (i + k) % 4) for i in range(4)]) for k in range(1, 4)
    ]
    far, far_rest, near = swap_fields(sent, head, rest)
    own_tail, near_tail, far_tail = sent, near, far
    kept, base = run(
        load_near_kernel,
        [((ROWS * SLOTS, B, B), bf16), (FULL, f32)],
        [
            (places_of, "s"), (fine_blocks, "h"), (sent, "v"), (near, "v"), (first, "v"),
            (ratio, "v"),
        ],
        [pltpu.SemaphoreType.DMA((TILE_ROWS,))],
        (NEAR_COST[0], 28_000_000),
    )

    def sweep_start(x, sent, near):
        return run(
            sweep_near_kernel,
            [(FULL, f32)],
            [(kept, "v"), (sent, "v"), (near, "v"), (x, "v"), (first, "v"), (ratio, "v")],
            cost=NEAR_COST,
        )[0]

    def sweep_end(far, far_rest, base):
        x, sent, head, rest = run(
            sweep_head_kernel,
            FIELDS,
            [(kept, "v"), (far, "v"), (base, "v"), (ratio, "v")],
            cost=HEAD_COST,
        )
        x, sent, head = run(
            sweep_rest_kernel,
            FIELDS[:3],
            [(kept, "v"), (far_rest, "v"), (ratio, "v"), (x, "v"), (sent, "v"), (head, "v")],
            cost=REST_COST,
            alias={3: 0, 4: 1, 5: 2},
        )
        return x, sent, head, rest

    x = first
    for turn in range(CYCLES):
        for _ in range(2 * (turn > 0)):
            far, far_rest, near = swap_fields(sent, head, rest)
            base = sweep_start(x, sent, near)
            x, sent, head, rest = sweep_end(far, far_rest, base)
        if turn == 0:
            x, sent, head, rest = sweep_end(far, far_rest, base)
        if turn == 0:
            far, near = swap_sides(sent)
        else:
            far, far_rest, near = swap_fields(sent, head, rest)
        (base,) = run(
            functools.partial(residual_near_kernel, turn == 0),
            [(FULL, f32)],
            [(kept, "v"), (sent, "v"), (near, "v"), (x, "v"), (right_side, "b"), (diag, "v")],
            cost=NEAR_COST,
        )
        if turn == 0:
            ops, scale = run(
                sort_kernel,
                [((12, B, B), bf16), (SIDE, f32)],
                [(p, "v") for p in pieces] + [(base, "v")],
            )
            res, side, sent = run(
                residual_far_kernel,
                [(FULL, f32), (SIDE, f32), (SIDE, bf16)],
                [(kept, "v"), (aggregate, "s"), (far, "v"), (base, "v"), (scale, "v")],
                cost=HEAD_COST,
            )
        else:
            res, side = run(
                residual_head_kernel,
                [(FULL, f32), (SIDE, f32)],
                [(kept, "v"), (aggregate, "s"), (far, "v"), (base, "v")],
                cost=HEAD_COST,
            )
            res, side, sent = run(
                residual_rest_kernel,
                [(FULL, f32), (SIDE, f32), (SIDE, bf16)],
                [
                    (kept, "v"), (own_tail, "v"), (far_rest, "v"), (scale, "v"), (res, "v"),
                    (side, "v"),
                ],
                cost=REST_COST,
                alias={4: 0, 5: 1},
            )
        far, near = swap_sides(sent)
        fix, sent = run(
            coarse_first_kernel,
            [(SIDE, f32), (SIDE, bf16)],
            [(ops, "v"), (side, "v"), (sent, "v"), (near, "v"), (far, "v")],
        )
        far, near = swap_sides(sent)
        (sent,) = run(
            coarse_second_kernel,
            [(SIDE, bf16)],
            [(ops, "v"), (side, "v"), (fix, "v"), (sent, "v"), (near, "v"), (far, "v")],
        )
        far, near = swap_sides(sent)
        (base,) = run(
            lift_near_kernel,
            [(FULL, f32)],
            [
                (kept, "v"), (aggregate, "s"), (sent, "v"), (near, "v"), (near_tail, "v"),
                (x, "v"), (res, "v"), (ratio, "v"),
            ],
            [pltpu.VMEM(FULL, bf16), pltpu.VMEM(FULL, bf16)],
            NEAR_COST,
        )
        x, sent, head, rest = run(
            lift_far_kernel,
            FIELDS,
            [(kept, "v"), (far, "v"), (far_tail, "v"), (base, "v"), (ratio, "v")],
            [pltpu.VMEM(FULL, bf16)],
            (10 * TILE_FLOPS, 3_000_000),
        )
        far, far_rest, near = swap_fields(sent, head, rest)
        base = sweep_start(x, sent, near)
        if turn < CYCLES - 1:
            x, sent, head, rest = sweep_end(far, far_rest, base)
    (x,) = run(
        last_head_kernel,
        [(FULL, f32)],
        [(kept, "v"), (far, "v"), (base, "v"), (ratio, "v")],
        cost=HEAD_COST,
    )
    (x,) = run(
        last_rest_kernel,
        [(FULL, f32)],
        [(kept, "v"), (far_rest, "v"), (ratio, "v"), (x, "v")],
        [pltpu.VMEM(REST, f32), pltpu.SemaphoreType.DMA((TILE_ROWS,))],
        REST_COST,
        hbm_outs=(0,),
    )
    return x


def solution(mesh):
    in_specs = (
        P("rows", "rhs"),
        P("rows", None, None, None),
        P("rows", None),
        P("rows"),
        P("rows"),
        P(("rhs", "rows"), None, None, None),
        P(("rhs", "rows")),
    )
    return jax.shard_map(
        shards, mesh=mesh, in_specs=in_specs, out_specs=P("rows", "rhs"), check_vma=False
    )
```

time: 157 us -> 154 us (0.981)
  waiting for transfers between devices: 48.6 us -> 24 us
  starting transfers between devices: 42 us -> 57.7 us
  Pallas kernels: 65.1 us -> 71.9 us
    ppermute x26 -> x32, waiting for transfers between devices: 47.4 us -> 22.7 us  [the longest x19 22.7 us: swap_far(): return lax.ppermute(x, 'rows', pairs)]
    ppermute x26 -> x32, starting transfers between devices: 37.3 us -> 53 us  [the longest x19 52.3 us: swap_far(): return lax.ppermute(x, 'rows', pairs)]
    pallas_call x25 -> x30, Pallas kernels: 65.1 us -> 71.9 us  [run(): pl.pallas_call(kernel, out_shape=[jax.ShapeDtypeStruct(shape, dtype) if n...]
  transfers between devices with their start and end apart: 29 -> 35, of which waited for: 12 -> 12; matrix products, arithmetic and copies ran while one was open for 0% -> 0% of each run, Pallas kernels for 29% -> 39%
where the time goes in v1:
time: 154 us
  Pallas kernels  71.9 us (47%)
  starting transfers between devices  57.7 us (37%)
  waiting for transfers between devices  24 us (16%)
    pallas_call x30, Pallas kernels, run(): pl.pallas_call(kernel, out_shape=[jax.ShapeDtypeStruct(shape, dtype) if n...  71.9 us
    ppermute x19, starting transfers between devices, swap_far(): return lax.ppermute(x, 'rows', pairs)  52.3 us
    ppermute x19, waiting for transfers between devices, swap_far(): return lax.ppermute(x, 'rows', pairs)  22.7 us
    ppermute x3, starting transfers between devices, shards(): lax.ppermute(packed, 'rhs', [(i, (i + k) % 4) for i in range(4)])  4.62 us
  transfers between devices with their start and end apart: 35, of which 12 were waited for; matrix products, arithmetic and copies ran while one was open for 0% of the time, Pallas kernels for 39%

profile of v1, /device:TPU:0, one launch (start us, length us, event | category | flops | bytes accessed | tf_op | source)
XLA Modules:
  0.0 154.1 jit_solution(4332071605447327332)
XLA Ops:
  2.0 6.4 %collective-permute-start.5 = (bf16[1552,128]{1,0:T(8,128)(2,1)S(1)}, bf16[1552,128]{1,0:T(8,128)(2,1)S(1)}, u32[]{:S(2)}, u32[]{:S(2)}) collective-permute-start(bf16[1552,128]{1,0:T(8,128)(2,1)S(1)} %get-tuple-element.70), channel_id=1, source_target_pairs={{0,31},{1,2},{2,1},{3,4},{4,3},{5,6},{6,5},{7,8},{8,7},{9,10},{10,... | collective-permute-start | bytes 1191944 | tf_op jit(solution)/shard_map/ppermute | solution.py:534
  8.5 8.7 %shard_map.74 = (bf16[576,128,128]{2,1,0:T(8,128)(2,1)S(1)}, f32[2048,128]{1,0:T(8,128)S(1)}) custom-call(s32[16,128]{1,0:T(8,128)S(1)} %get-tuple-element.63.places_ref, bf16[16,32,128,128]{3,2,1,0:T(8,128)(2,1)} %blocks_ref.1, bf16[2064,128]{1,0:T(8,128)(2,1)S(1)} %get-tuple-element.64.own_ref.tail_ref, ...), custom_call_target="tpu_custom_call" | custom-call | flops 1744830464 | bytes 28000000 | tf_op jit(solution)/shard_map/pallas_call | solution.py:513
  19.6 5.1 %collective-permute-start.7 = (bf16[2048,128]{1,0:T(8,128)(2,1)S(1)}, bf16[2048,128]{1,0:T(8,128)(2,1)S(1)}, u32[]{:S(2)}, u32[]{:S(2)}) collective-permute-start(bf16[2048,128]{1,0:T(8,128)(2,1)S(1)} %get-tuple-element.75.own_ref), channel_id=1, source_target_pairs={{0,31},{1,2},{2,1},{3,4},{4,3},{5,6},{6,5},{7,8},{8,7},{9,10},{10,... | collective-permute-start | bytes 1572872 | tf_op jit(solution)/shard_map/ppermute | solution.py:534
  24.7 3.0 %collective-permute-start.3 = (bf16[400,128]{1,0:T(8,128)(2,1)S(1)}, bf16[400,128]{1,0:T(8,128)(2,1)S(1)}, u32[]{:S(2)}, u32[]{:S(2)}) collective-permute-start(bf16[400,128]{1,0:T(8,128)(2,1)S(1)} %get-tuple-element.68.p0_ref), channel_id=1, source_target_pairs={{0,96},{32,0},{64,32},{96,64},{1,97},{33,1},{65,33},{97,65},{2,98}... | collective-permute-start | bytes 307208 | tf_op jit(solution)/shard_map/ppermute | solution.py:581
  29.3 4.4 %shard_map.77.after_ref.base_ref = f32[2048,128]{1,0:T(8,128)S(1)} custom-call(bf16[576,128,128]{2,1,0:T(8,128)(2,1)S(1)} %get-tuple-element.67.kept_ref, bf16[2048,128]{1,0:T(8,128)(2,1)S(1)} %get-tuple-element.75.own_ref, bf16[2048,128]{1,0:T(8,128)(2,1)S(1)} %collective-permute-done.6.near_ref, f32[2048,128]{1,0:T(8,128)S(1)} %get-tuple-element.76.x_ref, ...), custom_call_target="tpu_custom_call" | custom-call | flops 1744830464 | bytes 8000000 | tf_op jit(solution)/shard_map/pallas_call | solution.py:513
  38.8 6.2 %collective-permute-done.9.far_ref = bf16[512,128]{1,0:T(8,128)(2,1)S(1)} collective-permute-done((bf16[512,128]{1,0:T(8,128)(2,1)S(1)}, bf16[512,128]{1,0:T(8,128)(2,1)S(1)}, u32[]{:S(2)}, u32[]{:S(2)}) %collective-permute-start.9) | collective-permute-done | bytes 131104 | tf_op jit(solution)/shard_map/ppermute | solution.py:534
  46.9 6.2 %collective-permute-done.11.far_ref = bf16[512,128]{1,0:T(8,128)(2,1)S(1)} collective-permute-done((bf16[512,128]{1,0:T(8,128)(2,1)S(1)}, bf16[512,128]{1,0:T(8,128)(2,1)S(1)}, u32[]{:S(2)}, u32[]{:S(2)}) %collective-permute-start.11) | collective-permute-done | bytes 131104 | tf_op jit(solution)/shard_map/ppermute | solution.py:534
  55.3 5.9 %shard_map.82.base_ref = f32[2048,128]{1,0:T(8,128)S(1)} custom-call(bf16[576,128,128]{2,1,0:T(8,128)(2,1)S(1)} %get-tuple-element.67.kept_ref, s32[16]{0:T(128)S(1)} %copy-done.1, bf16[512,128]{1,0:T(8,128)(2,1)S(1)} %shard_map.81.coarse_ref, bf16[512,128]{1,0:T(8,128)(2,1)S(1)} %collective-permute-done.13.near_ref, ...), custom_call_target="tpu_custom_call" | custom-call | flops 1744830464 | bytes 8000000 | tf_op jit(solution)/shard_map/pallas_call | solution.py:513
  63.3 3.4 %collective-permute-start.14 = (bf16[1536,128]{1,0:T(8,128)(2,1)S(1)}, bf16[1536,128]{1,0:T(8,128)(2,1)S(1)}, u32[]{:S(2)}, u32[]{:S(2)}) collective-permute-start(bf16[1536,128]{1,0:T(8,128)(2,1)S(1)} %get-tuple-element.85), channel_id=1, source_target_pairs={{0,31},{1,2},{2,1},{3,4},{4,3},{5,6},{6,5},{7,8},{8,7},{9,10},{10,... | collective-permute-start | bytes 1179656 | tf_op jit(solution)/shard_map/ppermute | solution.py:534
  68.4 5.3 %shard_map.84.base_ref = f32[2048,128]{1,0:T(8,128)S(1)} custom-call(bf16[576,128,128]{2,1,0:T(8,128)(2,1)S(1)} %get-tuple-element.67.kept_ref, bf16[2048,128]{1,0:T(8,128)(2,1)S(1)} %get-tuple-element.86.own_ref, bf16[2048,128]{1,0:T(8,128)(2,1)S(1)} %collective-permute-done.15.near_ref, f32[2048,128]{1,0:T(8,128)S(1)} %get-tuple-element.87.x_ref, ...), custom_call_target="tpu_custom_call" | custom-call | flops 1744830464 | bytes 8000000 | tf_op jit(solution)/shard_map/pallas_call | solution.py:513
  75.7 3.4 %collective-permute-start.18 = (bf16[1536,128]{1,0:T(8,128)(2,1)S(1)}, bf16[1536,128]{1,0:T(8,128)(2,1)S(1)}, u32[]{:S(2)}, u32[]{:S(2)}) collective-permute-start(bf16[1536,128]{1,0:T(8,128)(2,1)S(1)} %get-tuple-element.93), channel_id=1, source_target_pairs={{0,31},{1,2},{2,1},{3,4},{4,3},{5,6},{6,5},{7,8},{8,7},{9,10},{10,... | collective-permute-start | bytes 1179656 | tf_op jit(solution)/shard_map/ppermute | solution.py:534
  80.8 5.3 %shard_map.87.base_ref = f32[2048,128]{1,0:T(8,128)S(1)} custom-call(bf16[576,128,128]{2,1,0:T(8,128)(2,1)S(1)} %get-tuple-element.67.kept_ref, bf16[2048,128]{1,0:T(8,128)(2,1)S(1)} %get-tuple-element.94.own_ref, bf16[2048,128]{1,0:T(8,128)(2,1)S(1)} %collective-permute-done.19.near_ref, f32[2048,128]{1,0:T(8,128)S(1)} %get-tuple-element.95.x_ref, ...), custom_call_target="tpu_custom_call" | custom-call | flops 1744830464 | bytes 8000000 | tf_op jit(solution)/shard_map/pallas_call | solution.py:513
  88.1 3.4 %collective-permute-start.20 = (bf16[1536,128]{1,0:T(8,128)(2,1)S(1)}, bf16[1536,128]{1,0:T(8,128)(2,1)S(1)}, u32[]{:S(2)}, u32[]{:S(2)}) collective-permute-start(bf16[1536,128]{1,0:T(8,128)(2,1)S(1)} %get-tuple-element.99), channel_id=1, source_target_pairs={{0,31},{1,2},{2,1},{3,4},{4,3},{5,6},{6,5},{7,8},{8,7},{9,10},{10,... | collective-permute-start | bytes 1179656 | tf_op jit(solution)/shard_map/ppermute | solution.py:534
  93.3 5.3 %shard_map.90.base_ref = f32[2048,128]{1,0:T(8,128)S(1)} custom-call(bf16[576,128,128]{2,1,0:T(8,128)(2,1)S(1)} %get-tuple-element.67.kept_ref, bf16[2048,128]{1,0:T(8,128)(2,1)S(1)} %get-tuple-element.100.own_ref, bf16[2048,128]{1,0:T(8,128)(2,1)S(1)} %collective-permute-done.21.near_ref, f32[2048,128]{1,0:T(8,128)S(1)} %get-tuple-element.101.x_ref, ...), custom_call_target="tpu_custom_call" | custom-call | flops 1744830464 | bytes 8000000 | tf_op jit(solution)/shard_map/pallas_call | solution.py:513
  100.5 3.4 %collective-permute-start.24 = (bf16[1536,128]{1,0:T(8,128)(2,1)S(1)}, bf16[1536,128]{1,0:T(8,128)(2,1)S(1)}, u32[]{:S(2)}, u32[]{:S(2)}) collective-permute-start(bf16[1536,128]{1,0:T(8,128)(2,1)S(1)} %get-tuple-element.107), channel_id=1, source_target_pairs={{0,31},{1,2},{2,1},{3,4},{4,3},{5,6},{6,5},{7,8},{8,7},{9,10},{10,... | collective-permute-start | bytes 1179656 | tf_op jit(solution)/shard_map/ppermute | solution.py:534
  105.7 5.2 %shard_map.93.base_ref = f32[2048,128]{1,0:T(8,128)S(1)} custom-call(bf16[576,128,128]{2,1,0:T(8,128)(2,1)S(1)} %get-tuple-element.67.kept_ref, bf16[2048,128]{1,0:T(8,128)(2,1)S(1)} %get-tuple-element.108.own_ref, bf16[2048,128]{1,0:T(8,128)(2,1)S(1)} %collective-permute-done.25.near_ref, f32[2048,128]{1,0:T(8,128)S(1)} %get-tuple-element.109.x_ref, ...), custom_call_target="tpu_custom_call" | custom-call | flops 1744830464 | bytes 8000000 | tf_op jit(solution)/shard_map/pallas_call | solution.py:513
  113.5 3.4 %collective-permute-start.27 = (bf16[512,128]{1,0:T(8,128)(2,1)S(1)}, bf16[512,128]{1,0:T(8,128)(2,1)S(1)}, u32[]{:S(2)}, u32[]{:S(2)}) collective-permute-start(bf16[512,128]{1,0:T(8,128)(2,1)S(1)} %get-tuple-element.113.own_ref), channel_id=1, source_target_pairs={{0,31},{1,2},{2,1},{3,4},{4,3},{5,6},{6,5},{7,8},{8,7},{9,10},{10,... | collective-permute-start | bytes 393224 | tf_op jit(solution)/shard_map/ppermute | solution.py:534
  116.8 4.4 %collective-permute-done.27.far_ref = bf16[512,128]{1,0:T(8,128)(2,1)S(1)} collective-permute-done((bf16[512,128]{1,0:T(8,128)(2,1)S(1)}, bf16[512,128]{1,0:T(8,128)(2,1)S(1)}, u32[]{:S(2)}, u32[]{:S(2)}) %collective-permute-start.27) | collective-permute-done | bytes 131104 | tf_op jit(solution)/shard_map/ppermute | solution.py:534
  121.5 3.4 %collective-permute-start.29 = (bf16[512,128]{1,0:T(8,128)(2,1)S(1)}, bf16[512,128]{1,0:T(8,128)(2,1)S(1)}, u32[]{:S(2)}, u32[]{:S(2)}) collective-permute-start(bf16[512,128]{1,0:T(8,128)(2,1)S(1)} %get-tuple-element.115.own_ref), channel_id=1, source_target_pairs={{0,31},{1,2},{2,1},{3,4},{4,3},{5,6},{6,5},{7,8},{8,7},{9,10},{10,... | collective-permute-start | bytes 393224 | tf_op jit(solution)/shard_map/ppermute | solution.py:534
  124.9 4.4 %collective-permute-done.29.far_ref = bf16[512,128]{1,0:T(8,128)(2,1)S(1)} collective-permute-done((bf16[512,128]{1,0:T(8,128)(2,1)S(1)}, bf16[512,128]{1,0:T(8,128)(2,1)S(1)}, u32[]{:S(2)}, u32[]{:S(2)}) %collective-permute-start.29) | collective-permute-done | bytes 131104 | tf_op jit(solution)/shard_map/ppermute | solution.py:534
  129.7 3.4 %collective-permute-start.30 = (bf16[512,128]{1,0:T(8,128)(2,1)S(1)}, bf16[512,128]{1,0:T(8,128)(2,1)S(1)}, u32[]{:S(2)}, u32[]{:S(2)}) collective-permute-start(bf16[512,128]{1,0:T(8,128)(2,1)S(1)} %shard_map.97.coarse_ref), channel_id=1, source_target_pairs={{0,31},{1,2},{2,1},{3,4},{4,3},{5,6},{6,5},{7,8},{8,7},{9,10},{10,... | collective-permute-start | bytes 393224 | tf_op jit(solution)/shard_map/ppermute | solution.py:534
  133.1 5.9 %shard_map.98.base_ref = f32[2048,128]{1,0:T(8,128)S(1)} custom-call(bf16[576,128,128]{2,1,0:T(8,128)(2,1)S(1)} %get-tuple-element.67.kept_ref, s32[16]{0:T(128)S(1)} %copy-done.1, bf16[512,128]{1,0:T(8,128)(2,1)S(1)} %shard_map.97.coarse_ref, bf16[512,128]{1,0:T(8,128)(2,1)S(1)} %collective-permute-done.31.near_ref, ...), custom_call_target="tpu_custom_call" | custom-call | flops 1744830464 | bytes 8000000 | tf_op jit(solution)/shard_map/pallas_call | solution.py:513
  142.7 3.3 %collective-permute-start.32 = (bf16[512,128]{1,0:T(8,128)(2,1)S(1)}, bf16[512,128]{1,0:T(8,128)(2,1)S(1)}, u32[]{:S(2)}, u32[]{:S(2)}) collective-permute-start(bf16[512,128]{1,0:T(8,128)(2,1)S(1)} %get-tuple-element.117), channel_id=1, source_target_pairs={{0,31},{1,2},{2,1},{3,4},{4,3},{5,6},{6,5},{7,8},{8,7},{9,10},{10,... | collective-permute-start | bytes 393224 | tf_op jit(solution)/shard_map/ppermute | solution.py:534
  145.9 5.2 %shard_map.100.base_ref = f32[2048,128]{1,0:T(8,128)S(1)} custom-call(bf16[576,128,128]{2,1,0:T(8,128)(2,1)S(1)} %get-tuple-element.67.kept_ref, bf16[2048,128]{1,0:T(8,128)(2,1)S(1)} %get-tuple-element.119.own_ref, bf16[2048,128]{1,0:T(8,128)(2,1)S(1)} %collective-permute-done.34.near_ref, f32[2048,128]{1,0:T(8,128)S(1)} %get-tuple-element.120.x_ref, ...), custom_call_target="tpu_custom_call" | custom-call | flops 1744830464 | bytes 8000000 | tf_op jit(solution)/shard_map/pallas_call | solution.py:513
  (80 shorter events, 39.8 us)
Async XLA Ops:
  1.9 6.6 %collective-permute-start = (bf16[2064,128]{1,0:T(8,128)(2,1)S(1)}, bf16[2064,128]{1,0:T(8,128)(2,1)S(1)}, u32[]{:S(2)}, u32[]{:S(2)}) collective-permute-start(bf16[2064,128]{1,0:T(8,128)(2,1)S(1)} %get-tuple-element.64.own_ref.tail_ref), channel_id=1, source_target_pairs={{0,1},{1,0},{2,3},{3,2},{4,5},{5,4},{6,7},{7,6},{8,9},{9,8},{10,11... | collective-permute-start | bytes 1585160 | tf_op jit(solution)/shard_map/ppermute | solution.py:529
  2.0 15.2 %collective-permute-start.5 = (bf16[1552,128]{1,0:T(8,128)(2,1)S(1)}, bf16[1552,128]{1,0:T(8,128)(2,1)S(1)}, u32[]{:S(2)}, u32[]{:S(2)}) collective-permute-start(bf16[1552,128]{1,0:T(8,128)(2,1)S(1)} %get-tuple-element.70), channel_id=1, source_target_pairs={{0,31},{1,2},{2,1},{3,4},{4,3},{5,6},{6,5},{7,8},{8,7},{9,10},{10,... | collective-permute-start | bytes 1191944 | tf_op jit(solution)/shard_map/ppermute | solution.py:534
  8.4 10.7 %collective-permute-start.4 = (bf16[512,128]{1,0:T(8,128)(2,1)S(1)}, bf16[512,128]{1,0:T(8,128)(2,1)S(1)}, u32[]{:S(2)}, u32[]{:S(2)}) collective-permute-start(bf16[512,128]{1,0:T(8,128)(2,1)S(1)} %get-tuple-element.69), channel_id=1, source_target_pairs={{0,31},{1,2},{2,1},{3,4},{4,3},{5,6},{6,5},{7,8},{8,7},{9,10},{10,... | collective-permute-start | bytes 393224 | tf_op jit(solution)/shard_map/ppermute | solution.py:534
  19.5 9.8 %collective-permute-start.6 = (bf16[2048,128]{1,0:T(8,128)(2,1)S(1)}, bf16[2048,128]{1,0:T(8,128)(2,1)S(1)}, u32[]{:S(2)}, u32[]{:S(2)}) collective-permute-start(bf16[2048,128]{1,0:T(8,128)(2,1)S(1)} %get-tuple-element.75.own_ref), channel_id=1, source_target_pairs={{0,1},{1,0},{2,3},{3,2},{4,5},{5,4},{6,7},{7,6},{8,9},{9,8},{10,11... | collective-permute-start | bytes 1572872 | tf_op jit(solution)/shard_map/ppermute | solution.py:529
  19.6 15.5 %collective-permute-start.7 = (bf16[2048,128]{1,0:T(8,128)(2,1)S(1)}, bf16[2048,128]{1,0:T(8,128)(2,1)S(1)}, u32[]{:S(2)}, u32[]{:S(2)}) collective-permute-start(bf16[2048,128]{1,0:T(8,128)(2,1)S(1)} %get-tuple-element.75.own_ref), channel_id=1, source_target_pairs={{0,31},{1,2},{2,1},{3,4},{4,3},{5,6},{6,5},{7,8},{8,7},{9,10},{10,... | collective-permute-start | bytes 1572872 | tf_op jit(solution)/shard_map/ppermute | solution.py:534
  24.7 9.0 %collective-permute-start.3 = (bf16[400,128]{1,0:T(8,128)(2,1)S(1)}, bf16[400,128]{1,0:T(8,128)(2,1)S(1)}, u32[]{:S(2)}, u32[]{:S(2)}) collective-permute-start(bf16[400,128]{1,0:T(8,128)(2,1)S(1)} %get-tuple-element.68.p0_ref), channel_id=1, source_target_pairs={{0,96},{32,0},{64,32},{96,64},{1,97},{33,1},{65,33},{97,65},{2,98}... | collective-permute-start | bytes 307208 | tf_op jit(solution)/shard_map/ppermute | solution.py:581
  27.7 6.2 %collective-permute-start.2 = (bf16[400,128]{1,0:T(8,128)(2,1)S(1)}, bf16[400,128]{1,0:T(8,128)(2,1)S(1)}, u32[]{:S(2)}, u32[]{:S(2)}) collective-permute-start(bf16[400,128]{1,0:T(8,128)(2,1)S(1)} %get-tuple-element.68.p0_ref), channel_id=1, source_target_pairs={{0,64},{32,96},{64,0},{96,32},{1,65},{33,97},{65,1},{97,33},{2,66}... | collective-permute-start | bytes 307208 | tf_op jit(solution)/shard_map/ppermute | solution.py:581
  28.3 6.6 %collective-permute-start.1 = (bf16[400,128]{1,0:T(8,128)(2,1)S(1)}, bf16[400,128]{1,0:T(8,128)(2,1)S(1)}, u32[]{:S(2)}, u32[]{:S(2)}) collective-permute-start(bf16[400,128]{1,0:T(8,128)(2,1)S(1)} %get-tuple-element.68.p0_ref), channel_id=1, source_target_pairs={{0,32},{32,64},{64,96},{96,0},{1,33},{33,65},{65,97},{97,1},{2,34}... | collective-permute-start | bytes 307208 | tf_op jit(solution)/shard_map/ppermute | solution.py:581
  37.3 7.8 %collective-permute-start.9 = (bf16[512,128]{1,0:T(8,128)(2,1)S(1)}, bf16[512,128]{1,0:T(8,128)(2,1)S(1)}, u32[]{:S(2)}, u32[]{:S(2)}) collective-permute-start(bf16[512,128]{1,0:T(8,128)(2,1)S(1)} %get-tuple-element.81.own_ref), channel_id=1, source_target_pairs={{0,31},{1,2},{2,1},{3,4},{4,3},{5,6},{6,5},{7,8},{8,7},{9,10},{10,... | collective-permute-start | bytes 393224 | tf_op jit(solution)/shard_map/ppermute | solution.py:534
  45.4 7.8 %collective-permute-start.11 = (bf16[512,128]{1,0:T(8,128)(2,1)S(1)}, bf16[512,128]{1,0:T(8,128)(2,1)S(1)}, u32[]{:S(2)}, u32[]{:S(2)}) collective-permute-start(bf16[512,128]{1,0:T(8,128)(2,1)S(1)} %get-tuple-element.83.own_ref), channel_id=1, source_target_pairs={{0,31},{1,2},{2,1},{3,4},{4,3},{5,6},{6,5},{7,8},{8,7},{9,10},{10,... | collective-permute-start | bytes 393224 | tf_op jit(solution)/shard_map/ppermute | solution.py:534
  53.5 8.0 %collective-permute-start.12 = (bf16[512,128]{1,0:T(8,128)(2,1)S(1)}, bf16[512,128]{1,0:T(8,128)(2,1)S(1)}, u32[]{:S(2)}, u32[]{:S(2)}) collective-permute-start(bf16[512,128]{1,0:T(8,128)(2,1)S(1)} %shard_map.81.coarse_ref), channel_id=1, source_target_pairs={{0,31},{1,2},{2,1},{3,4},{4,3},{5,6},{6,5},{7,8},{8,7},{9,10},{10,... | collective-permute-start | bytes 393224 | tf_op jit(solution)/shard_map/ppermute | solution.py:534
  63.3 10.6 %collective-permute-start.14 = (bf16[1536,128]{1,0:T(8,128)(2,1)S(1)}, bf16[1536,128]{1,0:T(8,128)(2,1)S(1)}, u32[]{:S(2)}, u32[]{:S(2)}) collective-permute-start(bf16[1536,128]{1,0:T(8,128)(2,1)S(1)} %get-tuple-element.85), channel_id=1, source_target_pairs={{0,31},{1,2},{2,1},{3,4},{4,3},{5,6},{6,5},{7,8},{8,7},{9,10},{10,... | collective-permute-start | bytes 1179656 | tf_op jit(solution)/shard_map/ppermute | solution.py:534
  66.6 8.7 %collective-permute-start.17 = (bf16[512,128]{1,0:T(8,128)(2,1)S(1)}, bf16[512,128]{1,0:T(8,128)(2,1)S(1)}, u32[]{:S(2)}, u32[]{:S(2)}) collective-permute-start(bf16[512,128]{1,0:T(8,128)(2,1)S(1)} %get-tuple-element.89), channel_id=1, source_target_pairs={{0,31},{1,2},{2,1},{3,4},{4,3},{5,6},{6,5},{7,8},{8,7},{9,10},{10,... | collective-permute-start | bytes 393224 | tf_op jit(solution)/shard_map/ppermute | solution.py:534
  75.7 10.6 %collective-permute-start.18 = (bf16[1536,128]{1,0:T(8,128)(2,1)S(1)}, bf16[1536,128]{1,0:T(8,128)(2,1)S(1)}, u32[]{:S(2)}, u32[]{:S(2)}) collective-permute-start(bf16[1536,128]{1,0:T(8,128)(2,1)S(1)} %get-tuple-element.93), channel_id=1, source_target_pairs={{0,31},{1,2},{2,1},{3,4},{4,3},{5,6},{6,5},{7,8},{8,7},{9,10},{10,... | collective-permute-start | bytes 1179656 | tf_op jit(solution)/shard_map/ppermute | solution.py:534
  79.1 8.7 %collective-permute-start.16 = (bf16[512,128]{1,0:T(8,128)(2,1)S(1)}, bf16[512,128]{1,0:T(8,128)(2,1)S(1)}, u32[]{:S(2)}, u32[]{:S(2)}) collective-permute-start(bf16[512,128]{1,0:T(8,128)(2,1)S(1)} %get-tuple-element.88), channel_id=1, source_target_pairs={{0,31},{1,2},{2,1},{3,4},{4,3},{5,6},{6,5},{7,8},{8,7},{9,10},{10,... | collective-permute-start | bytes 393224 | tf_op jit(solution)/shard_map/ppermute | solution.py:534
  88.1 10.6 %collective-permute-start.20 = (bf16[1536,128]{1,0:T(8,128)(2,1)S(1)}, bf16[1536,128]{1,0:T(8,128)(2,1)S(1)}, u32[]{:S(2)}, u32[]{:S(2)}) collective-permute-start(bf16[1536,128]{1,0:T(8,128)(2,1)S(1)} %get-tuple-element.99), channel_id=1, source_target_pairs={{0,31},{1,2},{2,1},{3,4},{4,3},{5,6},{6,5},{7,8},{8,7},{9,10},{10,... | collective-permute-start | bytes 1179656 | tf_op jit(solution)/shard_map/ppermute | solution.py:534
  91.5 8.7 %collective-permute-start.23 = (bf16[512,128]{1,0:T(8,128)(2,1)S(1)}, bf16[512,128]{1,0:T(8,128)(2,1)S(1)}, u32[]{:S(2)}, u32[]{:S(2)}) collective-permute-start(bf16[512,128]{1,0:T(8,128)(2,1)S(1)} %get-tuple-element.103), channel_id=1, source_target_pairs={{0,31},{1,2},{2,1},{3,4},{4,3},{5,6},{6,5},{7,8},{8,7},{9,10},{10,... | collective-permute-start | bytes 393224 | tf_op jit(solution)/shard_map/ppermute | solution.py:534
  100.5 10.6 %collective-permute-start.24 = (bf16[1536,128]{1,0:T(8,128)(2,1)S(1)}, bf16[1536,128]{1,0:T(8,128)(2,1)S(1)}, u32[]{:S(2)}, u32[]{:S(2)}) collective-permute-start(bf16[1536,128]{1,0:T(8,128)(2,1)S(1)} %get-tuple-element.107), channel_id=1, source_target_pairs={{0,31},{1,2},{2,1},{3,4},{4,3},{5,6},{6,5},{7,8},{8,7},{9,10},{10,... | collective-permute-start | bytes 1179656 | tf_op jit(solution)/shard_map/ppermute | solution.py:534
  103.9 9.2 %collective-permute-start.22 = (bf16[512,128]{1,0:T(8,128)(2,1)S(1)}, bf16[512,128]{1,0:T(8,128)(2,1)S(1)}, u32[]{:S(2)}, u32[]{:S(2)}) collective-permute-start(bf16[512,128]{1,0:T(8,128)(2,1)S(1)} %get-tuple-element.102), channel_id=1, source_target_pairs={{0,31},{1,2},{2,1},{3,4},{4,3},{5,6},{6,5},{7,8},{8,7},{9,10},{10,... | collective-permute-start | bytes 393224 | tf_op jit(solution)/shard_map/ppermute | solution.py:534
  113.5 7.8 %collective-permute-start.27 = (bf16[512,128]{1,0:T(8,128)(2,1)S(1)}, bf16[512,128]{1,0:T(8,128)(2,1)S(1)}, u32[]{:S(2)}, u32[]{:S(2)}) collective-permute-start(bf16[512,128]{1,0:T(8,128)(2,1)S(1)} %get-tuple-element.113.own_ref), channel_id=1, source_target_pairs={{0,31},{1,2},{2,1},{3,4},{4,3},{5,6},{6,5},{7,8},{8,7},{9,10},{10,... | collective-permute-start | bytes 393224 | tf_op jit(solution)/shard_map/ppermute | solution.py:534
  121.5 7.8 %collective-permute-start.29 = (bf16[512,128]{1,0:T(8,128)(2,1)S(1)}, bf16[512,128]{1,0:T(8,128)(2,1)S(1)}, u32[]{:S(2)}, u32[]{:S(2)}) collective-permute-start(bf16[512,128]{1,0:T(8,128)(2,1)S(1)} %get-tuple-element.115.own_ref), channel_id=1, source_target_pairs={{0,31},{1,2},{2,1},{3,4},{4,3},{5,6},{6,5},{7,8},{8,7},{9,10},{10,... | collective-permute-start | bytes 393224 | tf_op jit(solution)/shard_map/ppermute | solution.py:534
  129.7 9.3 %collective-permute-start.30 = (bf16[512,128]{1,0:T(8,128)(2,1)S(1)}, bf16[512,128]{1,0:T(8,128)(2,1)S(1)}, u32[]{:S(2)}, u32[]{:S(2)}) collective-permute-start(bf16[512,128]{1,0:T(8,128)(2,1)S(1)} %shard_map.97.coarse_ref), channel_id=1, source_target_pairs={{0,31},{1,2},{2,1},{3,4},{4,3},{5,6},{6,5},{7,8},{8,7},{9,10},{10,... | collective-permute-start | bytes 393224 | tf_op jit(solution)/shard_map/ppermute | solution.py:534
  140.8 10.6 %collective-permute-start.33 = (bf16[1536,128]{1,0:T(8,128)(2,1)S(1)}, bf16[1536,128]{1,0:T(8,128)(2,1)S(1)}, u32[]{:S(2)}, u32[]{:S(2)}) collective-permute-start(bf16[1536,128]{1,0:T(8,128)(2,1)S(1)} %get-tuple-element.118), channel_id=1, source_target_pairs={{0,31},{1,2},{2,1},{3,4},{4,3},{5,6},{6,5},{7,8},{8,7},{9,10},{10,... | collective-permute-start | bytes 1179656 | tf_op jit(solution)/shard_map/ppermute | solution.py:534
  142.7 10.2 %collective-permute-start.32 = (bf16[512,128]{1,0:T(8,128)(2,1)S(1)}, bf16[512,128]{1,0:T(8,128)(2,1)S(1)}, u32[]{:S(2)}, u32[]{:S(2)}) collective-permute-start(bf16[512,128]{1,0:T(8,128)(2,1)S(1)} %get-tuple-element.117), channel_id=1, source_target_pairs={{0,31},{1,2},{2,1},{3,4},{4,3},{5,6},{6,5},{7,8},{8,7},{9,10},{10,... | collective-permute-start | bytes 393224 | tf_op jit(solution)/shard_map/ppermute | solution.py:534
  (13 other events, 80.9 us)

commit v2 on v1

--- a/solution.py
+++ b/solution.py
@@ -468,7 +468,9 @@
     return out
 
 
-def coarse_first_kernel(ops_ref, side_ref, own_ref, near_ref, far_ref, fix_ref, sent_ref):
+def coarse_first_kernel(
+    ops_ref, side_ref, own_ref, near_ref, far_ref, fix_ref, sent_ref, ops_out_ref
+):
     keep, gain = ratios()[0]
 
     def emit(rows, part):
@@ -478,6 +480,8 @@
         sent_ref[rows, :] = fix.astype(bf16)
 
     coarse_terms(ops_ref, own_ref, near_ref, far_ref, emit)
+    for n in range(12):
+        ops_out_ref[pl.ds(n * B, B), :] = ops_ref[n]
 
 
 def coarse_second_kernel(ops_ref, side_ref, fix_ref, own_ref, near_ref, far_ref, sent_ref):
@@ -490,6 +494,84 @@
         sent_ref[rows, :] = fix.astype(bf16)
 
     coarse_terms(ops_ref, own_ref, near_ref, far_ref, emit)
+
+
+def join_kernel(own_ref, near_ref, out_ref):
+    out_ref[pl.ds(0, QROWS), :] = own_ref[...]
+    out_ref[pl.ds(QROWS, QROWS), :] = near_ref[...]
+
+
+def coarse_wide_kernel(
+    ops_ref, near_ops_ref, far_ops_ref, side_ref, own_ref, near_ref, far_ref, beyond_ref, sent_ref,
+    near_s, far_s, fix_s,
+):
+    i = lax.axis_index("rows")
+    last = lax.axis_size("rows") - 1
+    near_dir = jnp.where(core_of() == 0, 2, 0)
+    far_dir = 2 - near_dir
+    far_step = (i == last).astype(jnp.int32) - (i == 0).astype(jnp.int32)
+    beyond_step = (i == last - 1).astype(jnp.int32) - (i == 1).astype(jnp.int32)
+    keep, gain = ratios()[0]
+    keep_next, gain_next = ratios()[1]
+
+    def at(q, step):
+        return jnp.clip(q + step, 0, 3)
+
+    def inside(q, step):
+        return jnp.logical_and(q + step >= 0, q + step <= 3).astype(f32)
+
+    def block(ref, q, step=None, start=0):
+        if step is None:
+            return ref[pl.ds(start + q * B, B), :]
+        value = ref[pl.ds(pl.multiple_of(start + at(q, step) * B, B), B), :]
+        return (inside(q, step) * value.astype(f32)).astype(bf16)
+
+    def product(ops, fields):
+        return jnp.dot(
+            jnp.concatenate(ops, axis=1),
+            jnp.concatenate(fields, axis=0),
+            preferred_element_type=f32,
+        )
+
+    for q in range(4):
+        rows = pl.ds(q * B, B)
+        own, near, far = block(own_ref, q), block(near_ref, q), block(far_ref, q, far_step)
+        part = product(
+            [ops_ref[q * 3 + far_dir], ops_ref[q * 3 + 1], ops_ref[q * 3 + near_dir]],
+            [far, own, near],
+        )
+        side = side_ref[rows, :] / THETA
+        fix_s[rows, :] = side + keep * side + gain * (side_ref[rows, :] - side - part)
+        ops = [near_ops_ref[pl.ds((q * 3 + d) * B, B), :] for d in range(3)]
+        lower_is_own = (near_dir == 2).astype(f32)
+        beyond = block(beyond_ref, q, beyond_step).astype(f32)
+        own_f = own.astype(f32)
+        low = (lower_is_own * own_f + (1.0 - lower_is_own) * beyond).astype(bf16)
+        high = (lower_is_own * beyond + (1.0 - lower_is_own) * own_f).astype(bf16)
+        part = product(ops, [low, near, high])
+        value = near.astype(f32)
+        side = value / THETA
+        near_s[rows, :] = (side + keep * side + gain * (value - side - part)).astype(bf16)
+        first = pl.multiple_of(at(q, far_step) * 3 * B, B)
+        ops = [far_ops_ref[pl.ds(pl.multiple_of(first + d * B, B), B), :] for d in range(3)]
+        outer = block(far_ref, q, far_step, QROWS).astype(f32)
+        low = (lower_is_own * outer + (1.0 - lower_is_own) * own_f).astype(bf16)
+        high = (lower_is_own * own_f + (1.0 - lower_is_own) * outer).astype(bf16)
+        part = product(ops, [low, far, high])
+        value = far.astype(f32)
+        side = value / THETA
+        fix = side + keep * side + gain * (value - side - part)
+        far_s[rows, :] = (inside(q, far_step) * fix).astype(bf16)
+    for q in range(4):
+        rows = pl.ds(q * B, B)
+        fix = fix_s[rows, :]
+        part = product(
+            [ops_ref[q * 3 + far_dir], ops_ref[q * 3 + 1], ops_ref[q * 3 + near_dir]],
+            [far_s[rows, :], fix.astype(bf16), near_s[rows, :]],
+        )
+        update = fix - side_ref[rows, :] / THETA
+        fix = fix + keep_next * update + gain_next * (side_ref[rows, :] - fix - part)
+        sent_ref[rows, :] = fix.astype(bf16)
 
 
 def run(kernel, outs, args, scratch=(), cost=(0, 0), hbm_outs=(), alias={}):
@@ -664,18 +746,34 @@
                 cost=REST_COST,
                 alias={4: 0, 5: 1},
             )
-        far, near = swap_sides(sent)
-        fix, sent = run(
-            coarse_first_kernel,
-            [(SIDE, f32), (SIDE, bf16)],
-            [(ops, "v"), (side, "v"), (sent, "v"), (near, "v"), (far, "v")],
-        )
-        far, near = swap_sides(sent)
-        (sent,) = run(
-            coarse_second_kernel,
-            [(SIDE, bf16)],
-            [(ops, "v"), (side, "v"), (fix, "v"), (sent, "v"), (near, "v"), (far, "v")],
-        )
+        if turn == 0:
+            far, near = swap_sides(sent)
+            fix, sent, ops_sent = run(
+                coarse_first_kernel,
+                [(SIDE, f32), (SIDE, bf16), ((12 * B, B), bf16)],
+                [(ops, "v"), (side, "v"), (sent, "v"), (near, "v"), (far, "v")],
+            )
+            far, near = swap_sides(sent)
+            far_ops, near_ops = swap_sides(ops_sent)
+            (sent,) = run(
+                coarse_second_kernel,
+                [(SIDE, bf16)],
+                [(ops, "v"), (side, "v"), (fix, "v"), (sent, "v"), (near, "v"), (far, "v")],
+            )
+        else:
+            near = swap_near(sent, size)
+            (pair,) = run(join_kernel, [((2 * QROWS, B), bf16)], [(sent, "v"), (near, "v")])
+            far = swap_far(pair, size)
+            beyond = swap_near(far, size)
+            (sent,) = run(
+                coarse_wide_kernel,
+                [(SIDE, bf16)],
+                [
+                    (ops, "v"), (near_ops, "v"), (far_ops, "v"), (side, "v"), (sent, "v"),
+                    (near, "v"), (far, "v"), (beyond, "v"),
+                ],
+                [pltpu.VMEM(SIDE, bf16), pltpu.VMEM(SIDE, bf16), pltpu.VMEM(SIDE, f32)],
+            )
         far, near = swap_sides(sent)
         (base,) = run(
             lift_near_kernel,

time: 154 us -> 154 us (level)
    ppermute x19, starting transfers between devices: 52.3 us -> 50.3 us  [swap_far(): return lax.ppermute(x, 'rows', pairs)]
  transfers between devices with their start and end apart: 35 -> 36, of which waited for: 12 -> 11; matrix products, arithmetic and copies ran while one was open for 0% -> 0% of each run, Pallas kernels for 39% -> 40%
where the time goes in v2:
time: 154 us
  Pallas kernels  72.1 us (47%)
  starting transfers between devices  57.1 us (37%)
  waiting for transfers between devices  23.8 us (15%)
    pallas_call x30, Pallas kernels, run(): pl.pallas_call(kernel, out_shape=[jax.ShapeDtypeStruct(shape, dtype) if n...  72.1 us
    ppermute x19, starting transfers between devices, swap_far(): return lax.ppermute(x, 'rows', pairs)  50.3 us
    ppermute x19, waiting for transfers between devices, swap_far(): return lax.ppermute(x, 'rows', pairs)  22.5 us
    ppermute x3, starting transfers between devices, shards(): lax.ppermute(packed, 'rhs', [(i, (i + k) % 4) for i in range(4)])  5.83 us
  transfers between devices with their start and end apart: 36, of which 11 were waited for; matrix products, arithmetic and copies ran while one was open for 0% of the time, Pallas kernels for 40%

profile of v2, /device:TPU:0, one launch (start us, length us, event | category | flops | bytes accessed | tf_op | source)
XLA Modules:
  0.0 153.7 jit_solution(10109192633849850550)
XLA Ops:
  2.0 6.4 %collective-permute-start.5 = (bf16[1552,128]{1,0:T(8,128)(2,1)S(1)}, bf16[1552,128]{1,0:T(8,128)(2,1)S(1)}, u32[]{:S(2)}, u32[]{:S(2)}) collective-permute-start(bf16[1552,128]{1,0:T(8,128)(2,1)S(1)} %get-tuple-element.69), channel_id=1, source_target_pairs={{0,31},{1,2},{2,1},{3,4},{4,3},{5,6},{6,5},{7,8},{8,7},{9,10},{10,... | collective-permute-start | bytes 1191944 | tf_op jit(solution)/shard_map/ppermute | solution.py:616
  8.5 8.7 %shard_map.74 = (bf16[576,128,128]{2,1,0:T(8,128)(2,1)S(1)}, f32[2048,128]{1,0:T(8,128)S(1)}) custom-call(s32[16,128]{1,0:T(8,128)S(1)} %get-tuple-element.62.places_ref, bf16[16,32,128,128]{3,2,1,0:T(8,128)(2,1)} %blocks_ref.1, bf16[2064,128]{1,0:T(8,128)(2,1)S(1)} %get-tuple-element.63.own_ref.tail_ref, ...), custom_call_target="tpu_custom_call" | custom-call | flops 1744830464 | bytes 28000000 | tf_op jit(solution)/shard_map/pallas_call | solution.py:595
  19.6 5.1 %collective-permute-start.7 = (bf16[2048,128]{1,0:T(8,128)(2,1)S(1)}, bf16[2048,128]{1,0:T(8,128)(2,1)S(1)}, u32[]{:S(2)}, u32[]{:S(2)}) collective-permute-start(bf16[2048,128]{1,0:T(8,128)(2,1)S(1)} %get-tuple-element.74.own_ref), channel_id=1, source_target_pairs={{0,31},{1,2},{2,1},{3,4},{4,3},{5,6},{6,5},{7,8},{8,7},{9,10},{10,... | collective-permute-start | bytes 1572872 | tf_op jit(solution)/shard_map/ppermute | solution.py:616
  26.2 2.9 %collective-permute-start.2 = (bf16[400,128]{1,0:T(8,128)(2,1)S(1)}, bf16[400,128]{1,0:T(8,128)(2,1)S(1)}, u32[]{:S(2)}, u32[]{:S(2)}) collective-permute-start(bf16[400,128]{1,0:T(8,128)(2,1)S(1)} %get-tuple-element.67.p0_ref), channel_id=1, source_target_pairs={{0,64},{32,96},{64,0},{96,32},{1,65},{33,97},{65,1},{97,33},{2,66}... | collective-permute-start | bytes 307208 | tf_op jit(solution)/shard_map/ppermute | solution.py:663
  30.5 4.4 %shard_map.77.after_ref.base_ref = f32[2048,128]{1,0:T(8,128)S(1)} custom-call(bf16[576,128,128]{2,1,0:T(8,128)(2,1)S(1)} %get-tuple-element.66.kept_ref, bf16[2048,128]{1,0:T(8,128)(2,1)S(1)} %get-tuple-element.74.own_ref, bf16[2048,128]{1,0:T(8,128)(2,1)S(1)} %collective-permute-done.6.near_ref, f32[2048,128]{1,0:T(8,128)S(1)} %get-tuple-element.75.x_ref, ...), custom_call_target="tpu_custom_call" | custom-call | flops 1744830464 | bytes 8000000 | tf_op jit(solution)/shard_map/pallas_call | solution.py:595
  38.9 6.2 %collective-permute-done.9.far_ref = bf16[512,128]{1,0:T(8,128)(2,1)S(1)} collective-permute-done((bf16[512,128]{1,0:T(8,128)(2,1)S(1)}, bf16[512,128]{1,0:T(8,128)(2,1)S(1)}, u32[]{:S(2)}, u32[]{:S(2)}) %collective-permute-start.9) | collective-permute-done | bytes 131104 | tf_op jit(solution)/shard_map/ppermute | solution.py:616
  47.1 6.2 %collective-permute-done.13.far_ref = bf16[512,128]{1,0:T(8,128)(2,1)S(1)} collective-permute-done((bf16[512,128]{1,0:T(8,128)(2,1)S(1)}, bf16[512,128]{1,0:T(8,128)(2,1)S(1)}, u32[]{:S(2)}, u32[]{:S(2)}) %collective-permute-start.13) | collective-permute-done | bytes 131104 | tf_op jit(solution)/shard_map/ppermute | solution.py:616
  55.4 5.9 %shard_map.82.base_ref = f32[2048,128]{1,0:T(8,128)S(1)} custom-call(bf16[576,128,128]{2,1,0:T(8,128)(2,1)S(1)} %get-tuple-element.66.kept_ref, s32[16]{0:T(128)S(1)} %copy-done.1, bf16[512,128]{1,0:T(8,128)(2,1)S(1)} %shard_map.81.coarse_ref, bf16[512,128]{1,0:T(8,128)(2,1)S(1)} %collective-permute-done.15.near_ref, ...), custom_call_target="tpu_custom_call" | custom-call | flops 1744830464 | bytes 8000000 | tf_op jit(solution)/shard_map/pallas_call | solution.py:595
  63.4 3.4 %collective-permute-start.16 = (bf16[1536,128]{1,0:T(8,128)(2,1)S(1)}, bf16[1536,128]{1,0:T(8,128)(2,1)S(1)}, u32[]{:S(2)}, u32[]{:S(2)}) collective-permute-start(bf16[1536,128]{1,0:T(8,128)(2,1)S(1)} %get-tuple-element.85), channel_id=1, source_target_pairs={{0,31},{1,2},{2,1},{3,4},{4,3},{5,6},{6,5},{7,8},{8,7},{9,10},{10,... | collective-permute-start | bytes 1179656 | tf_op jit(solution)/shard_map/ppermute | solution.py:616
  68.6 5.3 %shard_map.84.base_ref = f32[2048,128]{1,0:T(8,128)S(1)} custom-call(bf16[576,128,128]{2,1,0:T(8,128)(2,1)S(1)} %get-tuple-element.66.kept_ref, bf16[2048,128]{1,0:T(8,128)(2,1)S(1)} %get-tuple-element.86.own_ref, bf16[2048,128]{1,0:T(8,128)(2,1)S(1)} %collective-permute-done.17.near_ref, f32[2048,128]{1,0:T(8,128)S(1)} %get-tuple-element.87.x_ref, ...), custom_call_target="tpu_custom_call" | custom-call | flops 1744830464 | bytes 8000000 | tf_op jit(solution)/shard_map/pallas_call | solution.py:595
  75.9 3.4 %collective-permute-start.20 = (bf16[1536,128]{1,0:T(8,128)(2,1)S(1)}, bf16[1536,128]{1,0:T(8,128)(2,1)S(1)}, u32[]{:S(2)}, u32[]{:S(2)}) collective-permute-start(bf16[1536,128]{1,0:T(8,128)(2,1)S(1)} %get-tuple-element.93), channel_id=1, source_target_pairs={{0,31},{1,2},{2,1},{3,4},{4,3},{5,6},{6,5},{7,8},{8,7},{9,10},{10,... | collective-permute-start | bytes 1179656 | tf_op jit(solution)/shard_map/ppermute | solution.py:616
  81.0 5.3 %shard_map.87.base_ref = f32[2048,128]{1,0:T(8,128)S(1)} custom-call(bf16[576,128,128]{2,1,0:T(8,128)(2,1)S(1)} %get-tuple-element.66.kept_ref, bf16[2048,128]{1,0:T(8,128)(2,1)S(1)} %get-tuple-element.94.own_ref, bf16[2048,128]{1,0:T(8,128)(2,1)S(1)} %collective-permute-done.21.near_ref, f32[2048,128]{1,0:T(8,128)S(1)} %get-tuple-element.95.x_ref, ...), custom_call_target="tpu_custom_call" | custom-call | flops 1744830464 | bytes 8000000 | tf_op jit(solution)/shard_map/pallas_call | solution.py:595
  88.3 3.4 %collective-permute-start.22 = (bf16[1536,128]{1,0:T(8,128)(2,1)S(1)}, bf16[1536,128]{1,0:T(8,128)(2,1)S(1)}, u32[]{:S(2)}, u32[]{:S(2)}) collective-permute-start(bf16[1536,128]{1,0:T(8,128)(2,1)S(1)} %get-tuple-element.99), channel_id=1, source_target_pairs={{0,31},{1,2},{2,1},{3,4},{4,3},{5,6},{6,5},{7,8},{8,7},{9,10},{10,... | collective-permute-start | bytes 1179656 | tf_op jit(solution)/shard_map/ppermute | solution.py:616
  93.4 5.3 %shard_map.90.base_ref = f32[2048,128]{1,0:T(8,128)S(1)} custom-call(bf16[576,128,128]{2,1,0:T(8,128)(2,1)S(1)} %get-tuple-element.66.kept_ref, bf16[2048,128]{1,0:T(8,128)(2,1)S(1)} %get-tuple-element.100.own_ref, bf16[2048,128]{1,0:T(8,128)(2,1)S(1)} %collective-permute-done.23.near_ref, f32[2048,128]{1,0:T(8,128)S(1)} %get-tuple-element.101.x_ref, ...), custom_call_target="tpu_custom_call" | custom-call | flops 1744830464 | bytes 8000000 | tf_op jit(solution)/shard_map/pallas_call | solution.py:595
  100.7 3.4 %collective-permute-start.26 = (bf16[1536,128]{1,0:T(8,128)(2,1)S(1)}, bf16[1536,128]{1,0:T(8,128)(2,1)S(1)}, u32[]{:S(2)}, u32[]{:S(2)}) collective-permute-start(bf16[1536,128]{1,0:T(8,128)(2,1)S(1)} %get-tuple-element.107), channel_id=1, source_target_pairs={{0,31},{1,2},{2,1},{3,4},{4,3},{5,6},{6,5},{7,8},{8,7},{9,10},{10,... | collective-permute-start | bytes 1179656 | tf_op jit(solution)/shard_map/ppermute | solution.py:616
  105.8 5.2 %shard_map.93.base_ref = f32[2048,128]{1,0:T(8,128)S(1)} custom-call(bf16[576,128,128]{2,1,0:T(8,128)(2,1)S(1)} %get-tuple-element.66.kept_ref, bf16[2048,128]{1,0:T(8,128)(2,1)S(1)} %get-tuple-element.108.own_ref, bf16[2048,128]{1,0:T(8,128)(2,1)S(1)} %collective-permute-done.27.near_ref, f32[2048,128]{1,0:T(8,128)S(1)} %get-tuple-element.109.x_ref, ...), custom_call_target="tpu_custom_call" | custom-call | flops 1744830464 | bytes 8000000 | tf_op jit(solution)/shard_map/pallas_call | solution.py:595
  115.1 3.4 %collective-permute-start.29 = (bf16[1024,128]{1,0:T(8,128)(2,1)S(1)}, bf16[1024,128]{1,0:T(8,128)(2,1)S(1)}, u32[]{:S(2)}, u32[]{:S(2)}) collective-permute-start(bf16[1024,128]{1,0:T(8,128)(2,1)S(1)} %shard_map.96), channel_id=1, source_target_pairs={{0,31},{1,2},{2,1},{3,4},{4,3},{5,6},{6,5},{7,8},{8,7},{9,10},{10,... | collective-permute-start | bytes 786440 | tf_op jit(solution)/shard_map/ppermute | solution.py:616
  120.2 4.0 %collective-permute-done.29.far_ref = bf16[1024,128]{1,0:T(8,128)(2,1)S(1)} collective-permute-done((bf16[1024,128]{1,0:T(8,128)(2,1)S(1)}, bf16[1024,128]{1,0:T(8,128)(2,1)S(1)}, u32[]{:S(2)}, u32[]{:S(2)}) %collective-permute-start.29) | collective-permute-done | bytes 262176 | tf_op jit(solution)/shard_map/ppermute | solution.py:616
  124.3 4.7 %collective-permute-done.11.far_ops_ref = bf16[1536,128]{1,0:T(8,128)(2,1)S(1)} collective-permute-done((bf16[1536,128]{1,0:T(8,128)(2,1)S(1)}, bf16[1536,128]{1,0:T(8,128)(2,1)S(1)}, u32[]{:S(2)}, u32[]{:S(2)}) %collective-permute-start.11) | collective-permute-done | bytes 393248 | tf_op jit(solution)/shard_map/ppermute | solution.py:616
  129.8 2.9 %collective-permute-start.31 = (bf16[512,128]{1,0:T(8,128)(2,1)S(1)}, bf16[512,128]{1,0:T(8,128)(2,1)S(1)}, u32[]{:S(2)}, u32[]{:S(2)}) collective-permute-start(bf16[512,128]{1,0:T(8,128)(2,1)S(1)} %shard_map.97.coarse_ref), channel_id=1, source_target_pairs={{0,31},{1,2},{2,1},{3,4},{4,3},{5,6},{6,5},{7,8},{8,7},{9,10},{10,... | collective-permute-start | bytes 393224 | tf_op jit(solution)/shard_map/ppermute | solution.py:616
  132.7 5.9 %shard_map.98.base_ref = f32[2048,128]{1,0:T(8,128)S(1)} custom-call(bf16[576,128,128]{2,1,0:T(8,128)(2,1)S(1)} %get-tuple-element.66.kept_ref, s32[16]{0:T(128)S(1)} %copy-done.1, bf16[512,128]{1,0:T(8,128)(2,1)S(1)} %shard_map.97.coarse_ref, bf16[512,128]{1,0:T(8,128)(2,1)S(1)} %collective-permute-done.32.near_ref, ...), custom_call_target="tpu_custom_call" | custom-call | flops 1744830464 | bytes 8000000 | tf_op jit(solution)/shard_map/pallas_call | solution.py:595
  140.4 2.3 %collective-permute-start.34 = (bf16[1536,128]{1,0:T(8,128)(2,1)S(1)}, bf16[1536,128]{1,0:T(8,128)(2,1)S(1)}, u32[]{:S(2)}, u32[]{:S(2)}) collective-permute-start(bf16[1536,128]{1,0:T(8,128)(2,1)S(1)} %get-tuple-element.116), channel_id=1, source_target_pairs={{0,31},{1,2},{2,1},{3,4},{4,3},{5,6},{6,5},{7,8},{8,7},{9,10},{10,... | collective-permute-start | bytes 1179656 | tf_op jit(solution)/shard_map/ppermute | solution.py:616
  142.7 2.8 %collective-permute-start.33 = (bf16[512,128]{1,0:T(8,128)(2,1)S(1)}, bf16[512,128]{1,0:T(8,128)(2,1)S(1)}, u32[]{:S(2)}, u32[]{:S(2)}) collective-permute-start(bf16[512,128]{1,0:T(8,128)(2,1)S(1)} %get-tuple-element.115), channel_id=1, source_target_pairs={{0,31},{1,2},{2,1},{3,4},{4,3},{5,6},{6,5},{7,8},{8,7},{9,10},{10,... | collective-permute-start | bytes 393224 | tf_op jit(solution)/shard_map/ppermute | solution.py:616
  145.5 5.2 %shard_map.100.base_ref = f32[2048,128]{1,0:T(8,128)S(1)} custom-call(bf16[576,128,128]{2,1,0:T(8,128)(2,1)S(1)} %get-tuple-element.66.kept_ref, bf16[2048,128]{1,0:T(8,128)(2,1)S(1)} %get-tuple-element.117.own_ref, bf16[2048,128]{1,0:T(8,128)(2,1)S(1)} %collective-permute-done.35.near_ref, f32[2048,128]{1,0:T(8,128)S(1)} %get-tuple-element.118.x_ref, ...), custom_call_target="tpu_custom_call" | custom-call | flops 1744830464 | bytes 8000000 | tf_op jit(solution)/shard_map/pallas_call | solution.py:595
  (82 shorter events, 41.6 us)
Async XLA Ops:
  1.9 6.6 %collective-permute-start = (bf16[2064,128]{1,0:T(8,128)(2,1)S(1)}, bf16[2064,128]{1,0:T(8,128)(2,1)S(1)}, u32[]{:S(2)}, u32[]{:S(2)}) collective-permute-start(bf16[2064,128]{1,0:T(8,128)(2,1)S(1)} %get-tuple-element.63.own_ref.tail_ref), channel_id=1, source_target_pairs={{0,1},{1,0},{2,3},{3,2},{4,5},{5,4},{6,7},{7,6},{8,9},{9,8},{10,11... | collective-permute-start | bytes 1585160 | tf_op jit(solution)/shard_map/ppermute | solution.py:611
  2.0 15.2 %collective-permute-start.5 = (bf16[1552,128]{1,0:T(8,128)(2,1)S(1)}, bf16[1552,128]{1,0:T(8,128)(2,1)S(1)}, u32[]{:S(2)}, u32[]{:S(2)}) collective-permute-start(bf16[1552,128]{1,0:T(8,128)(2,1)S(1)} %get-tuple-element.69), channel_id=1, source_target_pairs={{0,31},{1,2},{2,1},{3,4},{4,3},{5,6},{6,5},{7,8},{8,7},{9,10},{10,... | collective-permute-start | bytes 1191944 | tf_op jit(solution)/shard_map/ppermute | solution.py:616
  8.4 10.7 %collective-permute-start.4 = (bf16[512,128]{1,0:T(8,128)(2,1)S(1)}, bf16[512,128]{1,0:T(8,128)(2,1)S(1)}, u32[]{:S(2)}, u32[]{:S(2)}) collective-permute-start(bf16[512,128]{1,0:T(8,128)(2,1)S(1)} %get-tuple-element.68), channel_id=1, source_target_pairs={{0,31},{1,2},{2,1},{3,4},{4,3},{5,6},{6,5},{7,8},{8,7},{9,10},{10,... | collective-permute-start | bytes 393224 | tf_op jit(solution)/shard_map/ppermute | solution.py:616
  19.5 11.0 %collective-permute-start.6 = (bf16[2048,128]{1,0:T(8,128)(2,1)S(1)}, bf16[2048,128]{1,0:T(8,128)(2,1)S(1)}, u32[]{:S(2)}, u32[]{:S(2)}) collective-permute-start(bf16[2048,128]{1,0:T(8,128)(2,1)S(1)} %get-tuple-element.74.own_ref), channel_id=1, source_target_pairs={{0,1},{1,0},{2,3},{3,2},{4,5},{5,4},{6,7},{7,6},{8,9},{9,8},{10,11... | collective-permute-start | bytes 1572872 | tf_op jit(solution)/shard_map/ppermute | solution.py:611
  19.6 15.5 %collective-permute-start.7 = (bf16[2048,128]{1,0:T(8,128)(2,1)S(1)}, bf16[2048,128]{1,0:T(8,128)(2,1)S(1)}, u32[]{:S(2)}, u32[]{:S(2)}) collective-permute-start(bf16[2048,128]{1,0:T(8,128)(2,1)S(1)} %get-tuple-element.74.own_ref), channel_id=1, source_target_pairs={{0,31},{1,2},{2,1},{3,4},{4,3},{5,6},{6,5},{7,8},{8,7},{9,10},{10,... | collective-permute-start | bytes 1572872 | tf_op jit(solution)/shard_map/ppermute | solution.py:616
  24.7 10.2 %collective-permute-start.1 = (bf16[400,128]{1,0:T(8,128)(2,1)S(1)}, bf16[400,128]{1,0:T(8,128)(2,1)S(1)}, u32[]{:S(2)}, u32[]{:S(2)}) collective-permute-start(bf16[400,128]{1,0:T(8,128)(2,1)S(1)} %get-tuple-element.67.p0_ref), channel_id=1, source_target_pairs={{0,32},{32,64},{64,96},{96,0},{1,33},{33,65},{65,97},{97,1},{2,34}... | collective-permute-start | bytes 307208 | tf_op jit(solution)/shard_map/ppermute | solution.py:663
  26.2 8.7 %collective-permute-start.2 = (bf16[400,128]{1,0:T(8,128)(2,1)S(1)}, bf16[400,128]{1,0:T(8,128)(2,1)S(1)}, u32[]{:S(2)}, u32[]{:S(2)}) collective-permute-start(bf16[400,128]{1,0:T(8,128)(2,1)S(1)} %get-tuple-element.67.p0_ref), channel_id=1, source_target_pairs={{0,64},{32,96},{64,0},{96,32},{1,65},{33,97},{65,1},{97,33},{2,66}... | collective-permute-start | bytes 307208 | tf_op jit(solution)/shard_map/ppermute | solution.py:663
  37.3 7.8 %collective-permute-start.9 = (bf16[512,128]{1,0:T(8,128)(2,1)S(1)}, bf16[512,128]{1,0:T(8,128)(2,1)S(1)}, u32[]{:S(2)}, u32[]{:S(2)}) collective-permute-start(bf16[512,128]{1,0:T(8,128)(2,1)S(1)} %get-tuple-element.80.own_ref), channel_id=1, source_target_pairs={{0,31},{1,2},{2,1},{3,4},{4,3},{5,6},{6,5},{7,8},{8,7},{9,10},{10,... | collective-permute-start | bytes 393224 | tf_op jit(solution)/shard_map/ppermute | solution.py:616
  45.5 7.8 %collective-permute-start.13 = (bf16[512,128]{1,0:T(8,128)(2,1)S(1)}, bf16[512,128]{1,0:T(8,128)(2,1)S(1)}, u32[]{:S(2)}, u32[]{:S(2)}) collective-permute-start(bf16[512,128]{1,0:T(8,128)(2,1)S(1)} %get-tuple-element.83.own_ref), channel_id=1, source_target_pairs={{0,31},{1,2},{2,1},{3,4},{4,3},{5,6},{6,5},{7,8},{8,7},{9,10},{10,... | collective-permute-start | bytes 393224 | tf_op jit(solution)/shard_map/ppermute | solution.py:616
  53.7 8.0 %collective-permute-start.14 = (bf16[512,128]{1,0:T(8,128)(2,1)S(1)}, bf16[512,128]{1,0:T(8,128)(2,1)S(1)}, u32[]{:S(2)}, u32[]{:S(2)}) collective-permute-start(bf16[512,128]{1,0:T(8,128)(2,1)S(1)} %shard_map.81.coarse_ref), channel_id=1, source_target_pairs={{0,31},{1,2},{2,1},{3,4},{4,3},{5,6},{6,5},{7,8},{8,7},{9,10},{10,... | collective-permute-start | bytes 393224 | tf_op jit(solution)/shard_map/ppermute | solution.py:616
  63.4 10.6 %collective-permute-start.16 = (bf16[1536,128]{1,0:T(8,128)(2,1)S(1)}, bf16[1536,128]{1,0:T(8,128)(2,1)S(1)}, u32[]{:S(2)}, u32[]{:S(2)}) collective-permute-start(bf16[1536,128]{1,0:T(8,128)(2,1)S(1)} %get-tuple-element.85), channel_id=1, source_target_pairs={{0,31},{1,2},{2,1},{3,4},{4,3},{5,6},{6,5},{7,8},{8,7},{9,10},{10,... | collective-permute-start | bytes 1179656 | tf_op jit(solution)/shard_map/ppermute | solution.py:616
  66.8 8.7 %collective-permute-start.19 = (bf16[512,128]{1,0:T(8,128)(2,1)S(1)}, bf16[512,128]{1,0:T(8,128)(2,1)S(1)}, u32[]{:S(2)}, u32[]{:S(2)}) collective-permute-start(bf16[512,128]{1,0:T(8,128)(2,1)S(1)} %get-tuple-element.89), channel_id=1, source_target_pairs={{0,31},{1,2},{2,1},{3,4},{4,3},{5,6},{6,5},{7,8},{8,7},{9,10},{10,... | collective-permute-start | bytes 393224 | tf_op jit(solution)/shard_map/ppermute | solution.py:616
  75.9 10.6 %collective-permute-start.20 = (bf16[1536,128]{1,0:T(8,128)(2,1)S(1)}, bf16[1536,128]{1,0:T(8,128)(2,1)S(1)}, u32[]{:S(2)}, u32[]{:S(2)}) collective-permute-start(bf16[1536,128]{1,0:T(8,128)(2,1)S(1)} %get-tuple-element.93), channel_id=1, source_target_pairs={{0,31},{1,2},{2,1},{3,4},{4,3},{5,6},{6,5},{7,8},{8,7},{9,10},{10,... | collective-permute-start | bytes 1179656 | tf_op jit(solution)/shard_map/ppermute | solution.py:616
  79.2 8.7 %collective-permute-start.18 = (bf16[512,128]{1,0:T(8,128)(2,1)S(1)}, bf16[512,128]{1,0:T(8,128)(2,1)S(1)}, u32[]{:S(2)}, u32[]{:S(2)}) collective-permute-start(bf16[512,128]{1,0:T(8,128)(2,1)S(1)} %get-tuple-element.88), channel_id=1, source_target_pairs={{0,31},{1,2},{2,1},{3,4},{4,3},{5,6},{6,5},{7,8},{8,7},{9,10},{10,... | collective-permute-start | bytes 393224 | tf_op jit(solution)/shard_map/ppermute | solution.py:616
  88.3 10.6 %collective-permute-start.22 = (bf16[1536,128]{1,0:T(8,128)(2,1)S(1)}, bf16[1536,128]{1,0:T(8,128)(2,1)S(1)}, u32[]{:S(2)}, u32[]{:S(2)}) collective-permute-start(bf16[1536,128]{1,0:T(8,128)(2,1)S(1)} %get-tuple-element.99), channel_id=1, source_target_pairs={{0,31},{1,2},{2,1},{3,4},{4,3},{5,6},{6,5},{7,8},{8,7},{9,10},{10,... | collective-permute-start | bytes 1179656 | tf_op jit(solution)/shard_map/ppermute | solution.py:616
  91.6 8.7 %collective-permute-start.25 = (bf16[512,128]{1,0:T(8,128)(2,1)S(1)}, bf16[512,128]{1,0:T(8,128)(2,1)S(1)}, u32[]{:S(2)}, u32[]{:S(2)}) collective-permute-start(bf16[512,128]{1,0:T(8,128)(2,1)S(1)} %get-tuple-element.103), channel_id=1, source_target_pairs={{0,31},{1,2},{2,1},{3,4},{4,3},{5,6},{6,5},{7,8},{8,7},{9,10},{10,... | collective-permute-start | bytes 393224 | tf_op jit(solution)/shard_map/ppermute | solution.py:616
  100.7 10.6 %collective-permute-start.26 = (bf16[1536,128]{1,0:T(8,128)(2,1)S(1)}, bf16[1536,128]{1,0:T(8,128)(2,1)S(1)}, u32[]{:S(2)}, u32[]{:S(2)}) collective-permute-start(bf16[1536,128]{1,0:T(8,128)(2,1)S(1)} %get-tuple-element.107), channel_id=1, source_target_pairs={{0,31},{1,2},{2,1},{3,4},{4,3},{5,6},{6,5},{7,8},{8,7},{9,10},{10,... | collective-permute-start | bytes 1179656 | tf_op jit(solution)/shard_map/ppermute | solution.py:616
  104.1 9.2 %collective-permute-start.24 = (bf16[512,128]{1,0:T(8,128)(2,1)S(1)}, bf16[512,128]{1,0:T(8,128)(2,1)S(1)}, u32[]{:S(2)}, u32[]{:S(2)}) collective-permute-start(bf16[512,128]{1,0:T(8,128)(2,1)S(1)} %get-tuple-element.102), channel_id=1, source_target_pairs={{0,31},{1,2},{2,1},{3,4},{4,3},{5,6},{6,5},{7,8},{8,7},{9,10},{10,... | collective-permute-start | bytes 393224 | tf_op jit(solution)/shard_map/ppermute | solution.py:616
  115.1 9.2 %collective-permute-start.29 = (bf16[1024,128]{1,0:T(8,128)(2,1)S(1)}, bf16[1024,128]{1,0:T(8,128)(2,1)S(1)}, u32[]{:S(2)}, u32[]{:S(2)}) collective-permute-start(bf16[1024,128]{1,0:T(8,128)(2,1)S(1)} %shard_map.96), channel_id=1, source_target_pairs={{0,31},{1,2},{2,1},{3,4},{4,3},{5,6},{6,5},{7,8},{8,7},{9,10},{10,... | collective-permute-start | bytes 786440 | tf_op jit(solution)/shard_map/ppermute | solution.py:616
  118.4 5.9 %collective-permute-start.10 = (bf16[1536,128]{1,0:T(8,128)(2,1)S(1)}, bf16[1536,128]{1,0:T(8,128)(2,1)S(1)}, u32[]{:S(2)}, u32[]{:S(2)}) collective-permute-start(bf16[1536,128]{1,0:T(8,128)(2,1)S(1)} %get-tuple-element.81), channel_id=1, source_target_pairs={{0,1},{1,0},{2,3},{3,2},{4,5},{5,4},{6,7},{7,6},{8,9},{9,8},{10,11... | collective-permute-start | bytes 1179656 | tf_op jit(solution)/shard_map/ppermute | solution.py:611
  118.4 10.5 %collective-permute-start.11 = (bf16[1536,128]{1,0:T(8,128)(2,1)S(1)}, bf16[1536,128]{1,0:T(8,128)(2,1)S(1)}, u32[]{:S(2)}, u32[]{:S(2)}) collective-permute-start(bf16[1536,128]{1,0:T(8,128)(2,1)S(1)} %get-tuple-element.81), channel_id=1, source_target_pairs={{0,31},{1,2},{2,1},{3,4},{4,3},{5,6},{6,5},{7,8},{8,7},{9,10},{10,... | collective-permute-start | bytes 1179656 | tf_op jit(solution)/shard_map/ppermute | solution.py:616
  129.8 8.8 %collective-permute-start.31 = (bf16[512,128]{1,0:T(8,128)(2,1)S(1)}, bf16[512,128]{1,0:T(8,128)(2,1)S(1)}, u32[]{:S(2)}, u32[]{:S(2)}) collective-permute-start(bf16[512,128]{1,0:T(8,128)(2,1)S(1)} %shard_map.97.coarse_ref), channel_id=1, source_target_pairs={{0,31},{1,2},{2,1},{3,4},{4,3},{5,6},{6,5},{7,8},{8,7},{9,10},{10,... | collective-permute-start | bytes 393224 | tf_op jit(solution)/shard_map/ppermute | solution.py:616
  140.4 10.6 %collective-permute-start.34 = (bf16[1536,128]{1,0:T(8,128)(2,1)S(1)}, bf16[1536,128]{1,0:T(8,128)(2,1)S(1)}, u32[]{:S(2)}, u32[]{:S(2)}) collective-permute-start(bf16[1536,128]{1,0:T(8,128)(2,1)S(1)} %get-tuple-element.116), channel_id=1, source_target_pairs={{0,31},{1,2},{2,1},{3,4},{4,3},{5,6},{6,5},{7,8},{8,7},{9,10},{10,... | collective-permute-start | bytes 1179656 | tf_op jit(solution)/shard_map/ppermute | solution.py:616
  142.7 9.7 %collective-permute-start.33 = (bf16[512,128]{1,0:T(8,128)(2,1)S(1)}, bf16[512,128]{1,0:T(8,128)(2,1)S(1)}, u32[]{:S(2)}, u32[]{:S(2)}) collective-permute-start(bf16[512,128]{1,0:T(8,128)(2,1)S(1)} %get-tuple-element.115), channel_id=1, source_target_pairs={{0,31},{1,2},{2,1},{3,4},{4,3},{5,6},{6,5},{7,8},{8,7},{9,10},{10,... | collective-permute-start | bytes 393224 | tf_op jit(solution)/shard_map/ppermute | solution.py:616
  (14 other events, 75.6 us)

commit v3 on v2

--- a/solution.py
+++ b/solution.py
@@ -58,7 +58,7 @@
 
 def start_kernel(
     right_ref, diag_ref, group_ref, coarse_ref, coarse_diag_ref, columns_ref,
-    first_ref, sent_ref, head_ref, rest_ref, ratio_ref, diag_out_ref, packed_ref, places_ref,
+    first_ref, sent_ref, ratio_ref, diag_out_ref, packed_ref, places_ref,
     right_s, diag_s, group_s, coarse_s, coarse_diag_s, columns_s, sems,
 ):
     chunks = [
@@ -96,11 +96,6 @@
             ratio_ref[rows, :] = ratio
             first_ref[rows, :] = value
             sent_ref[rows, :] = value.astype(bf16)
-    even = core_of() == 0
-    head = pl.multiple_of(jnp.where(even, 0, TILE), TILE)
-    rest = pl.multiple_of(jnp.where(even, PIECE, 0), TILE)
-    head_ref[pl.ds(0, PIECE), :] = sent_ref[pl.ds(head, PIECE), :]
-    rest_ref[...] = sent_ref[pl.ds(rest, TILE), :]
     group_copy.wait()
     size = lax.axis_size("rows")
     index = lax.broadcasted_iota(jnp.int32, (TAIL, B), 0)
@@ -108,7 +103,6 @@
     for r in range(ROWS):
         tail = jnp.where(index == r, lax.div(group_s[r], size).astype(f32), tail)
     sent_ref[pl.ds(FIELD, TAIL), :] = tail.astype(bf16)
-    head_ref[pl.ds(PIECE, TAIL), :] = tail.astype(bf16)
 
 
 def pack(blocks_ref, diag_ref, out_ref):
@@ -274,6 +268,15 @@
     sweep_near(
         kept_ref, own_ref, near_ref, first_ref, first_ref, ratio_ref, base_ref, True, ready
     )
+
+
+def sweep_far_kernel(kept_ref, far_ref, base_ref, ratio_ref, x_ref, sent_ref):
+    def emit(m, rows, part):
+        value = base_ref[rows, :] - ratio_ref[rows, :] * part
+        x_ref[rows, :] = value
+        sent_ref[rows, :] = value.astype(bf16)
+
+    far_products(kept_ref, far_ref, emit)
 
 
 def sweep_head_kernel(kept_ref, far_ref, base_ref, ratio_ref, x_ref, sent_ref, head_ref, rest_ref):
@@ -418,7 +421,7 @@
 def lift_far_kernel(
     kept_ref, far_ref, far_tail_ref, base_ref, ratio_ref, x_ref, sent_ref, head_ref, rest_ref, far_s
 ):
-    spread(far_ref, far_tail_ref, PIECE, far_s)
+    spread(far_ref, far_tail_ref, FIELD, far_s)
 
     def emit(m, rows, part):
         value = base_ref[rows, :] - ratio_ref[rows, :] * part
@@ -630,10 +633,10 @@
 def shards(right_side, fine_blocks, fine_columns, fine_diag, aggregate, coarse_blocks, coarse_diag):
     size = lax.axis_size("rows")
 
-    first, sent, head, rest, ratio, diag, packed, places_of = run(
+    first, sent, ratio, diag, packed, places_of = run(
         start_kernel,
         [
-            (FULL, f32), ((FIELD + TAIL, B), bf16), ((PIECE + TAIL, B), bf16), (REST, bf16),
+            (FULL, f32), ((FIELD + TAIL, B), bf16),
             (FULL, f32), (FULL, f32), ((3 * B + TAIL, B), bf16),
             ((ROWS, B), jnp.int32),
         ],
@@ -662,7 +665,7 @@
     pieces = [packed] + [
         lax.ppermute(packed, "rhs", [(i, (i + k) % 4) for i in range(4)]) for k in range(1, 4)
     ]
-    far, far_rest, near = swap_fields(sent, head, rest)
+    far, near = swap_sides(sent)
     own_tail, near_tail, far_tail = sent, near, far
     kept, base = run(
         load_near_kernel,
@@ -706,7 +709,12 @@
             base = sweep_start(x, sent, near)
             x, sent, head, rest = sweep_end(far, far_rest, base)
         if turn == 0:
-            x, sent, head, rest = sweep_end(far, far_rest, base)
+            x, sent = run(
+                sweep_far_kernel,
+                FIELDS[:2],
+                [(kept, "v"), (far, "v"), (base, "v"), (ratio, "v")],
+                cost=HEAD_COST,
+            )
         if turn == 0:
             far, near = swap_sides(sent)
         else:

time: 154 us -> 151 us (0.981)
  starting transfers between devices: 57.1 us -> 55.3 us
    ppermute x19 -> x18, starting transfers between devices: 50.3 us -> 48.5 us  [swap_far(): return lax.ppermute(x, 'rows', pairs)]
    pallas_call x30 -> x29, Pallas kernels: 72.1 us -> 71.1 us  [run(): pl.pallas_call(kernel, out_shape=[jax.ShapeDtypeStruct(shape, dtype) if n...]
    ppermute x19 -> x18, waiting for transfers between devices: 22.5 us -> 22.6 us  [swap_far(): return lax.ppermute(x, 'rows', pairs)]
  transfers between devices with their start and end apart: 36 -> 35, of which waited for: 11 -> 11; matrix products, arithmetic and copies ran while one was open for 0% -> 0% of each run, Pallas kernels for 40% -> 39%
where the time goes in v3:
time: 151 us
  Pallas kernels  71.1 us (47%)
  starting transfers between devices  55.3 us (37%)
  waiting for transfers between devices  24 us (16%)
    pallas_call x29, Pallas kernels, run(): pl.pallas_call(kernel, out_shape=[jax.ShapeDtypeStruct(shape, dtype) if n...  71.1 us
    ppermute x18, starting transfers between devices, swap_far(): return lax.ppermute(x, 'rows', pairs)  48.5 us
    ppermute x18, waiting for transfers between devices, swap_far(): return lax.ppermute(x, 'rows', pairs)  22.6 us
    ppermute x3, starting transfers between devices, shards(): lax.ppermute(packed, 'rhs', [(i, (i + k) % 4) for i in range(4)])  5.82 us
  transfers between devices with their start and end apart: 35, of which 11 were waited for; matrix products, arithmetic and copies ran while one was open for 0% of the time, Pallas kernels for 39%

profile of v3, /device:TPU:0, one launch (start us, length us, event | category | flops | bytes accessed | tf_op | source)
XLA Modules:
  0.0 151.0 jit_solution(11945509447302201486)
XLA Ops:
  1.9 6.4 %collective-permute-start.4 = (bf16[2064,128]{1,0:T(8,128)(2,1)S(1)}, bf16[2064,128]{1,0:T(8,128)(2,1)S(1)}, u32[]{:S(2)}, u32[]{:S(2)}) collective-permute-start(bf16[2064,128]{1,0:T(8,128)(2,1)S(1)} %get-tuple-element.58.own_ref.tail_ref), channel_id=1, source_target_pairs={{0,31},{1,2},{2,1},{3,4},{4,3},{5,6},{6,5},{7,8},{8,7},{9,10},{10,... | collective-permute-start | bytes 1585160 | tf_op jit(solution)/shard_map/ppermute | solution.py:619
  8.3 8.7 %shard_map.74 = (bf16[576,128,128]{2,1,0:T(8,128)(2,1)S(1)}, f32[2048,128]{1,0:T(8,128)S(1)}) custom-call(s32[16,128]{1,0:T(8,128)S(1)} %get-tuple-element.57.places_ref, bf16[16,32,128,128]{3,2,1,0:T(8,128)(2,1)} %blocks_ref.1, bf16[2064,128]{1,0:T(8,128)(2,1)S(1)} %get-tuple-element.58.own_ref.tail_ref, ...), custom_call_target="tpu_custom_call" | custom-call | flops 1744830464 | bytes 28000000 | tf_op jit(solution)/shard_map/pallas_call | solution.py:598
  18.7 3.3 %collective-permute-start.6 = (bf16[2048,128]{1,0:T(8,128)(2,1)S(1)}, bf16[2048,128]{1,0:T(8,128)(2,1)S(1)}, u32[]{:S(2)}, u32[]{:S(2)}) collective-permute-start(bf16[2048,128]{1,0:T(8,128)(2,1)S(1)} %get-tuple-element.64.own_ref), channel_id=1, source_target_pairs={{0,31},{1,2},{2,1},{3,4},{4,3},{5,6},{6,5},{7,8},{8,7},{9,10},{10,... | collective-permute-start | bytes 1572872 | tf_op jit(solution)/shard_map/ppermute | solution.py:619
  23.6 2.9 %collective-permute-start.2 = (bf16[400,128]{1,0:T(8,128)(2,1)S(1)}, bf16[400,128]{1,0:T(8,128)(2,1)S(1)}, u32[]{:S(2)}, u32[]{:S(2)}) collective-permute-start(bf16[400,128]{1,0:T(8,128)(2,1)S(1)} %get-tuple-element.62.p0_ref), channel_id=1, source_target_pairs={{0,64},{32,96},{64,0},{96,32},{1,65},{33,97},{65,1},{97,33},{2,66}... | collective-permute-start | bytes 307208 | tf_op jit(solution)/shard_map/ppermute | solution.py:666
  27.8 4.4 %shard_map.76.after_ref.base_ref = f32[2048,128]{1,0:T(8,128)S(1)} custom-call(bf16[576,128,128]{2,1,0:T(8,128)(2,1)S(1)} %get-tuple-element.61.kept_ref, bf16[2048,128]{1,0:T(8,128)(2,1)S(1)} %get-tuple-element.64.own_ref, bf16[2048,128]{1,0:T(8,128)(2,1)S(1)} %collective-permute-done.5.near_ref, f32[2048,128]{1,0:T(8,128)S(1)} %get-tuple-element.65.x_ref, ...), custom_call_target="tpu_custom_call" | custom-call | flops 1744830464 | bytes 8000000 | tf_op jit(solution)/shard_map/pallas_call | solution.py:598
  36.3 6.2 %collective-permute-done.8.far_ref = bf16[512,128]{1,0:T(8,128)(2,1)S(1)} collective-permute-done((bf16[512,128]{1,0:T(8,128)(2,1)S(1)}, bf16[512,128]{1,0:T(8,128)(2,1)S(1)}, u32[]{:S(2)}, u32[]{:S(2)}) %collective-permute-start.8) | collective-permute-done | bytes 131104 | tf_op jit(solution)/shard_map/ppermute | solution.py:619
  44.4 6.2 %collective-permute-done.12.far_ref = bf16[512,128]{1,0:T(8,128)(2,1)S(1)} collective-permute-done((bf16[512,128]{1,0:T(8,128)(2,1)S(1)}, bf16[512,128]{1,0:T(8,128)(2,1)S(1)}, u32[]{:S(2)}, u32[]{:S(2)}) %collective-permute-start.12) | collective-permute-done | bytes 131104 | tf_op jit(solution)/shard_map/ppermute | solution.py:619
  52.8 5.9 %shard_map.81.base_ref = f32[2048,128]{1,0:T(8,128)S(1)} custom-call(bf16[576,128,128]{2,1,0:T(8,128)(2,1)S(1)} %get-tuple-element.61.kept_ref, s32[16]{0:T(128)S(1)} %copy-done.1, bf16[512,128]{1,0:T(8,128)(2,1)S(1)} %shard_map.80.coarse_ref, bf16[512,128]{1,0:T(8,128)(2,1)S(1)} %collective-permute-done.14.near_ref, ...), custom_call_target="tpu_custom_call" | custom-call | flops 1744830464 | bytes 8000000 | tf_op jit(solution)/shard_map/pallas_call | solution.py:598
  60.8 3.4 %collective-permute-start.15 = (bf16[1536,128]{1,0:T(8,128)(2,1)S(1)}, bf16[1536,128]{1,0:T(8,128)(2,1)S(1)}, u32[]{:S(2)}, u32[]{:S(2)}) collective-permute-start(bf16[1536,128]{1,0:T(8,128)(2,1)S(1)} %get-tuple-element.75), channel_id=1, source_target_pairs={{0,31},{1,2},{2,1},{3,4},{4,3},{5,6},{6,5},{7,8},{8,7},{9,10},{10,... | collective-permute-start | bytes 1179656 | tf_op jit(solution)/shard_map/ppermute | solution.py:619
  65.9 5.2 %shard_map.83.base_ref = f32[2048,128]{1,0:T(8,128)S(1)} custom-call(bf16[576,128,128]{2,1,0:T(8,128)(2,1)S(1)} %get-tuple-element.61.kept_ref, bf16[2048,128]{1,0:T(8,128)(2,1)S(1)} %get-tuple-element.76.own_ref, bf16[2048,128]{1,0:T(8,128)(2,1)S(1)} %collective-permute-done.16.near_ref, f32[2048,128]{1,0:T(8,128)S(1)} %get-tuple-element.77.x_ref, ...), custom_call_target="tpu_custom_call" | custom-call | flops 1744830464 | bytes 8000000 | tf_op jit(solution)/shard_map/pallas_call | solution.py:598
  73.2 3.4 %collective-permute-start.19 = (bf16[1536,128]{1,0:T(8,128)(2,1)S(1)}, bf16[1536,128]{1,0:T(8,128)(2,1)S(1)}, u32[]{:S(2)}, u32[]{:S(2)}) collective-permute-start(bf16[1536,128]{1,0:T(8,128)(2,1)S(1)} %get-tuple-element.83), channel_id=1, source_target_pairs={{0,31},{1,2},{2,1},{3,4},{4,3},{5,6},{6,5},{7,8},{8,7},{9,10},{10,... | collective-permute-start | bytes 1179656 | tf_op jit(solution)/shard_map/ppermute | solution.py:619
  78.3 5.2 %shard_map.86.base_ref = f32[2048,128]{1,0:T(8,128)S(1)} custom-call(bf16[576,128,128]{2,1,0:T(8,128)(2,1)S(1)} %get-tuple-element.61.kept_ref, bf16[2048,128]{1,0:T(8,128)(2,1)S(1)} %get-tuple-element.84.own_ref, bf16[2048,128]{1,0:T(8,128)(2,1)S(1)} %collective-permute-done.20.near_ref, f32[2048,128]{1,0:T(8,128)S(1)} %get-tuple-element.85.x_ref, ...), custom_call_target="tpu_custom_call" | custom-call | flops 1744830464 | bytes 8000000 | tf_op jit(solution)/shard_map/pallas_call | solution.py:598
  85.6 3.4 %collective-permute-start.21 = (bf16[1536,128]{1,0:T(8,128)(2,1)S(1)}, bf16[1536,128]{1,0:T(8,128)(2,1)S(1)}, u32[]{:S(2)}, u32[]{:S(2)}) collective-permute-start(bf16[1536,128]{1,0:T(8,128)(2,1)S(1)} %get-tuple-element.89), channel_id=1, source_target_pairs={{0,31},{1,2},{2,1},{3,4},{4,3},{5,6},{6,5},{7,8},{8,7},{9,10},{10,... | collective-permute-start | bytes 1179656 | tf_op jit(solution)/shard_map/ppermute | solution.py:619
  90.7 5.2 %shard_map.89.base_ref = f32[2048,128]{1,0:T(8,128)S(1)} custom-call(bf16[576,128,128]{2,1,0:T(8,128)(2,1)S(1)} %get-tuple-element.61.kept_ref, bf16[2048,128]{1,0:T(8,128)(2,1)S(1)} %get-tuple-element.90.own_ref, bf16[2048,128]{1,0:T(8,128)(2,1)S(1)} %collective-permute-done.22.near_ref, f32[2048,128]{1,0:T(8,128)S(1)} %get-tuple-element.91.x_ref, ...), custom_call_target="tpu_custom_call" | custom-call | flops 1744830464 | bytes 8000000 | tf_op jit(solution)/shard_map/pallas_call | solution.py:598
  98.0 3.4 %collective-permute-start.25 = (bf16[1536,128]{1,0:T(8,128)(2,1)S(1)}, bf16[1536,128]{1,0:T(8,128)(2,1)S(1)}, u32[]{:S(2)}, u32[]{:S(2)}) collective-permute-start(bf16[1536,128]{1,0:T(8,128)(2,1)S(1)} %get-tuple-element.97), channel_id=1, source_target_pairs={{0,31},{1,2},{2,1},{3,4},{4,3},{5,6},{6,5},{7,8},{8,7},{9,10},{10,... | collective-permute-start | bytes 1179656 | tf_op jit(solution)/shard_map/ppermute | solution.py:619
  103.2 5.2 %shard_map.92.base_ref = f32[2048,128]{1,0:T(8,128)S(1)} custom-call(bf16[576,128,128]{2,1,0:T(8,128)(2,1)S(1)} %get-tuple-element.61.kept_ref, bf16[2048,128]{1,0:T(8,128)(2,1)S(1)} %get-tuple-element.98.own_ref, bf16[2048,128]{1,0:T(8,128)(2,1)S(1)} %collective-permute-done.26.near_ref, f32[2048,128]{1,0:T(8,128)S(1)} %get-tuple-element.99.x_ref, ...), custom_call_target="tpu_custom_call" | custom-call | flops 1744830464 | bytes 8000000 | tf_op jit(solution)/shard_map/pallas_call | solution.py:598
  112.4 3.4 %collective-permute-start.28 = (bf16[1024,128]{1,0:T(8,128)(2,1)S(1)}, bf16[1024,128]{1,0:T(8,128)(2,1)S(1)}, u32[]{:S(2)}, u32[]{:S(2)}) collective-permute-start(bf16[1024,128]{1,0:T(8,128)(2,1)S(1)} %shard_map.95), channel_id=1, source_target_pairs={{0,31},{1,2},{2,1},{3,4},{4,3},{5,6},{6,5},{7,8},{8,7},{9,10},{10,... | collective-permute-start | bytes 786440 | tf_op jit(solution)/shard_map/ppermute | solution.py:619
  117.5 4.0 %collective-permute-done.28.far_ref = bf16[1024,128]{1,0:T(8,128)(2,1)S(1)} collective-permute-done((bf16[1024,128]{1,0:T(8,128)(2,1)S(1)}, bf16[1024,128]{1,0:T(8,128)(2,1)S(1)}, u32[]{:S(2)}, u32[]{:S(2)}) %collective-permute-start.28) | collective-permute-done | bytes 262176 | tf_op jit(solution)/shard_map/ppermute | solution.py:619
  121.6 4.7 %collective-permute-done.10.far_ops_ref = bf16[1536,128]{1,0:T(8,128)(2,1)S(1)} collective-permute-done((bf16[1536,128]{1,0:T(8,128)(2,1)S(1)}, bf16[1536,128]{1,0:T(8,128)(2,1)S(1)}, u32[]{:S(2)}, u32[]{:S(2)}) %collective-permute-start.10) | collective-permute-done | bytes 393248 | tf_op jit(solution)/shard_map/ppermute | solution.py:619
  127.1 2.9 %collective-permute-start.30 = (bf16[512,128]{1,0:T(8,128)(2,1)S(1)}, bf16[512,128]{1,0:T(8,128)(2,1)S(1)}, u32[]{:S(2)}, u32[]{:S(2)}) collective-permute-start(bf16[512,128]{1,0:T(8,128)(2,1)S(1)} %shard_map.96.coarse_ref), channel_id=1, source_target_pairs={{0,31},{1,2},{2,1},{3,4},{4,3},{5,6},{6,5},{7,8},{8,7},{9,10},{10,... | collective-permute-start | bytes 393224 | tf_op jit(solution)/shard_map/ppermute | solution.py:619
  130.0 5.9 %shard_map.97.base_ref = f32[2048,128]{1,0:T(8,128)S(1)} custom-call(bf16[576,128,128]{2,1,0:T(8,128)(2,1)S(1)} %get-tuple-element.61.kept_ref, s32[16]{0:T(128)S(1)} %copy-done.1, bf16[512,128]{1,0:T(8,128)(2,1)S(1)} %shard_map.96.coarse_ref, bf16[512,128]{1,0:T(8,128)(2,1)S(1)} %collective-permute-done.31.near_ref, ...), custom_call_target="tpu_custom_call" | custom-call | flops 1744830464 | bytes 8000000 | tf_op jit(solution)/shard_map/pallas_call | solution.py:598
  137.8 2.3 %collective-permute-start.33 = (bf16[1536,128]{1,0:T(8,128)(2,1)S(1)}, bf16[1536,128]{1,0:T(8,128)(2,1)S(1)}, u32[]{:S(2)}, u32[]{:S(2)}) collective-permute-start(bf16[1536,128]{1,0:T(8,128)(2,1)S(1)} %get-tuple-element.106), channel_id=1, source_target_pairs={{0,31},{1,2},{2,1},{3,4},{4,3},{5,6},{6,5},{7,8},{8,7},{9,10},{10,... | collective-permute-start | bytes 1179656 | tf_op jit(solution)/shard_map/ppermute | solution.py:619
  140.1 2.8 %collective-permute-start.32 = (bf16[512,128]{1,0:T(8,128)(2,1)S(1)}, bf16[512,128]{1,0:T(8,128)(2,1)S(1)}, u32[]{:S(2)}, u32[]{:S(2)}) collective-permute-start(bf16[512,128]{1,0:T(8,128)(2,1)S(1)} %get-tuple-element.105), channel_id=1, source_target_pairs={{0,31},{1,2},{2,1},{3,4},{4,3},{5,6},{6,5},{7,8},{8,7},{9,10},{10,... | collective-permute-start | bytes 393224 | tf_op jit(solution)/shard_map/ppermute | solution.py:619
  142.9 5.2 %shard_map.99.base_ref = f32[2048,128]{1,0:T(8,128)S(1)} custom-call(bf16[576,128,128]{2,1,0:T(8,128)(2,1)S(1)} %get-tuple-element.61.kept_ref, bf16[2048,128]{1,0:T(8,128)(2,1)S(1)} %get-tuple-element.107.own_ref, bf16[2048,128]{1,0:T(8,128)(2,1)S(1)} %collective-permute-done.34.near_ref, f32[2048,128]{1,0:T(8,128)S(1)} %get-tuple-element.108.x_ref, ...), custom_call_target="tpu_custom_call" | custom-call | flops 1744830464 | bytes 8000000 | tf_op jit(solution)/shard_map/pallas_call | solution.py:598
  (79 shorter events, 40.7 us)
Async XLA Ops:
  1.8 6.5 %collective-permute-start = (bf16[2064,128]{1,0:T(8,128)(2,1)S(1)}, bf16[2064,128]{1,0:T(8,128)(2,1)S(1)}, u32[]{:S(2)}, u32[]{:S(2)}) collective-permute-start(bf16[2064,128]{1,0:T(8,128)(2,1)S(1)} %get-tuple-element.58.own_ref.tail_ref), channel_id=1, source_target_pairs={{0,1},{1,0},{2,3},{3,2},{4,5},{5,4},{6,7},{7,6},{8,9},{9,8},{10,11... | collective-permute-start | bytes 1585160 | tf_op jit(solution)/shard_map/ppermute | solution.py:614
  1.9 15.2 %collective-permute-start.4 = (bf16[2064,128]{1,0:T(8,128)(2,1)S(1)}, bf16[2064,128]{1,0:T(8,128)(2,1)S(1)}, u32[]{:S(2)}, u32[]{:S(2)}) collective-permute-start(bf16[2064,128]{1,0:T(8,128)(2,1)S(1)} %get-tuple-element.58.own_ref.tail_ref), channel_id=1, source_target_pairs={{0,31},{1,2},{2,1},{3,4},{4,3},{5,6},{6,5},{7,8},{8,7},{9,10},{10,... | collective-permute-start | bytes 1585160 | tf_op jit(solution)/shard_map/ppermute | solution.py:619
  18.6 9.2 %collective-permute-start.5 = (bf16[2048,128]{1,0:T(8,128)(2,1)S(1)}, bf16[2048,128]{1,0:T(8,128)(2,1)S(1)}, u32[]{:S(2)}, u32[]{:S(2)}) collective-permute-start(bf16[2048,128]{1,0:T(8,128)(2,1)S(1)} %get-tuple-element.64.own_ref), channel_id=1, source_target_pairs={{0,1},{1,0},{2,3},{3,2},{4,5},{5,4},{6,7},{7,6},{8,9},{9,8},{10,11... | collective-permute-start | bytes 1572872 | tf_op jit(solution)/shard_map/ppermute | solution.py:614
  18.7 13.7 %collective-permute-start.6 = (bf16[2048,128]{1,0:T(8,128)(2,1)S(1)}, bf16[2048,128]{1,0:T(8,128)(2,1)S(1)}, u32[]{:S(2)}, u32[]{:S(2)}) collective-permute-start(bf16[2048,128]{1,0:T(8,128)(2,1)S(1)} %get-tuple-element.64.own_ref), channel_id=1, source_target_pairs={{0,31},{1,2},{2,1},{3,4},{4,3},{5,6},{6,5},{7,8},{8,7},{9,10},{10,... | collective-permute-start | bytes 1572872 | tf_op jit(solution)/shard_map/ppermute | solution.py:619
  22.0 10.2 %collective-permute-start.1 = (bf16[400,128]{1,0:T(8,128)(2,1)S(1)}, bf16[400,128]{1,0:T(8,128)(2,1)S(1)}, u32[]{:S(2)}, u32[]{:S(2)}) collective-permute-start(bf16[400,128]{1,0:T(8,128)(2,1)S(1)} %get-tuple-element.62.p0_ref), channel_id=1, source_target_pairs={{0,32},{32,64},{64,96},{96,0},{1,33},{33,65},{65,97},{97,1},{2,34}... | collective-permute-start | bytes 307208 | tf_op jit(solution)/shard_map/ppermute | solution.py:666
  23.6 8.6 %collective-permute-start.2 = (bf16[400,128]{1,0:T(8,128)(2,1)S(1)}, bf16[400,128]{1,0:T(8,128)(2,1)S(1)}, u32[]{:S(2)}, u32[]{:S(2)}) collective-permute-start(bf16[400,128]{1,0:T(8,128)(2,1)S(1)} %get-tuple-element.62.p0_ref), channel_id=1, source_target_pairs={{0,64},{32,96},{64,0},{96,32},{1,65},{33,97},{65,1},{97,33},{2,66}... | collective-permute-start | bytes 307208 | tf_op jit(solution)/shard_map/ppermute | solution.py:666
  26.5 5.8 %collective-permute-start.3 = (bf16[400,128]{1,0:T(8,128)(2,1)S(1)}, bf16[400,128]{1,0:T(8,128)(2,1)S(1)}, u32[]{:S(2)}, u32[]{:S(2)}) collective-permute-start(bf16[400,128]{1,0:T(8,128)(2,1)S(1)} %get-tuple-element.62.p0_ref), channel_id=1, source_target_pairs={{0,96},{32,0},{64,32},{96,64},{1,97},{33,1},{65,33},{97,65},{2,98}... | collective-permute-start | bytes 307208 | tf_op jit(solution)/shard_map/ppermute | solution.py:666
  34.7 7.8 %collective-permute-start.8 = (bf16[512,128]{1,0:T(8,128)(2,1)S(1)}, bf16[512,128]{1,0:T(8,128)(2,1)S(1)}, u32[]{:S(2)}, u32[]{:S(2)}) collective-permute-start(bf16[512,128]{1,0:T(8,128)(2,1)S(1)} %get-tuple-element.70.own_ref), channel_id=1, source_target_pairs={{0,31},{1,2},{2,1},{3,4},{4,3},{5,6},{6,5},{7,8},{8,7},{9,10},{10,... | collective-permute-start | bytes 393224 | tf_op jit(solution)/shard_map/ppermute | solution.py:619
  42.8 7.8 %collective-permute-start.12 = (bf16[512,128]{1,0:T(8,128)(2,1)S(1)}, bf16[512,128]{1,0:T(8,128)(2,1)S(1)}, u32[]{:S(2)}, u32[]{:S(2)}) collective-permute-start(bf16[512,128]{1,0:T(8,128)(2,1)S(1)} %get-tuple-element.73.own_ref), channel_id=1, source_target_pairs={{0,31},{1,2},{2,1},{3,4},{4,3},{5,6},{6,5},{7,8},{8,7},{9,10},{10,... | collective-permute-start | bytes 393224 | tf_op jit(solution)/shard_map/ppermute | solution.py:619
  51.0 8.0 %collective-permute-start.13 = (bf16[512,128]{1,0:T(8,128)(2,1)S(1)}, bf16[512,128]{1,0:T(8,128)(2,1)S(1)}, u32[]{:S(2)}, u32[]{:S(2)}) collective-permute-start(bf16[512,128]{1,0:T(8,128)(2,1)S(1)} %shard_map.80.coarse_ref), channel_id=1, source_target_pairs={{0,31},{1,2},{2,1},{3,4},{4,3},{5,6},{6,5},{7,8},{8,7},{9,10},{10,... | collective-permute-start | bytes 393224 | tf_op jit(solution)/shard_map/ppermute | solution.py:619
  60.8 10.6 %collective-permute-start.15 = (bf16[1536,128]{1,0:T(8,128)(2,1)S(1)}, bf16[1536,128]{1,0:T(8,128)(2,1)S(1)}, u32[]{:S(2)}, u32[]{:S(2)}) collective-permute-start(bf16[1536,128]{1,0:T(8,128)(2,1)S(1)} %get-tuple-element.75), channel_id=1, source_target_pairs={{0,31},{1,2},{2,1},{3,4},{4,3},{5,6},{6,5},{7,8},{8,7},{9,10},{10,... | collective-permute-start | bytes 1179656 | tf_op jit(solution)/shard_map/ppermute | solution.py:619
  64.1 8.6 %collective-permute-start.18 = (bf16[512,128]{1,0:T(8,128)(2,1)S(1)}, bf16[512,128]{1,0:T(8,128)(2,1)S(1)}, u32[]{:S(2)}, u32[]{:S(2)}) collective-permute-start(bf16[512,128]{1,0:T(8,128)(2,1)S(1)} %get-tuple-element.79), channel_id=1, source_target_pairs={{0,31},{1,2},{2,1},{3,4},{4,3},{5,6},{6,5},{7,8},{8,7},{9,10},{10,... | collective-permute-start | bytes 393224 | tf_op jit(solution)/shard_map/ppermute | solution.py:619
  73.2 10.6 %collective-permute-start.19 = (bf16[1536,128]{1,0:T(8,128)(2,1)S(1)}, bf16[1536,128]{1,0:T(8,128)(2,1)S(1)}, u32[]{:S(2)}, u32[]{:S(2)}) collective-permute-start(bf16[1536,128]{1,0:T(8,128)(2,1)S(1)} %get-tuple-element.83), channel_id=1, source_target_pairs={{0,31},{1,2},{2,1},{3,4},{4,3},{5,6},{6,5},{7,8},{8,7},{9,10},{10,... | collective-permute-start | bytes 1179656 | tf_op jit(solution)/shard_map/ppermute | solution.py:619
  76.6 8.6 %collective-permute-start.17 = (bf16[512,128]{1,0:T(8,128)(2,1)S(1)}, bf16[512,128]{1,0:T(8,128)(2,1)S(1)}, u32[]{:S(2)}, u32[]{:S(2)}) collective-permute-start(bf16[512,128]{1,0:T(8,128)(2,1)S(1)} %get-tuple-element.78), channel_id=1, source_target_pairs={{0,31},{1,2},{2,1},{3,4},{4,3},{5,6},{6,5},{7,8},{8,7},{9,10},{10,... | collective-permute-start | bytes 393224 | tf_op jit(solution)/shard_map/ppermute | solution.py:619
  85.6 10.6 %collective-permute-start.21 = (bf16[1536,128]{1,0:T(8,128)(2,1)S(1)}, bf16[1536,128]{1,0:T(8,128)(2,1)S(1)}, u32[]{:S(2)}, u32[]{:S(2)}) collective-permute-start(bf16[1536,128]{1,0:T(8,128)(2,1)S(1)} %get-tuple-element.89), channel_id=1, source_target_pairs={{0,31},{1,2},{2,1},{3,4},{4,3},{5,6},{6,5},{7,8},{8,7},{9,10},{10,... | collective-permute-start | bytes 1179656 | tf_op jit(solution)/shard_map/ppermute | solution.py:619
  89.0 8.6 %collective-permute-start.24 = (bf16[512,128]{1,0:T(8,128)(2,1)S(1)}, bf16[512,128]{1,0:T(8,128)(2,1)S(1)}, u32[]{:S(2)}, u32[]{:S(2)}) collective-permute-start(bf16[512,128]{1,0:T(8,128)(2,1)S(1)} %get-tuple-element.93), channel_id=1, source_target_pairs={{0,31},{1,2},{2,1},{3,4},{4,3},{5,6},{6,5},{7,8},{8,7},{9,10},{10,... | collective-permute-start | bytes 393224 | tf_op jit(solution)/shard_map/ppermute | solution.py:619
  98.0 10.6 %collective-permute-start.25 = (bf16[1536,128]{1,0:T(8,128)(2,1)S(1)}, bf16[1536,128]{1,0:T(8,128)(2,1)S(1)}, u32[]{:S(2)}, u32[]{:S(2)}) collective-permute-start(bf16[1536,128]{1,0:T(8,128)(2,1)S(1)} %get-tuple-element.97), channel_id=1, source_target_pairs={{0,31},{1,2},{2,1},{3,4},{4,3},{5,6},{6,5},{7,8},{8,7},{9,10},{10,... | collective-permute-start | bytes 1179656 | tf_op jit(solution)/shard_map/ppermute | solution.py:619
  101.4 9.2 %collective-permute-start.23 = (bf16[512,128]{1,0:T(8,128)(2,1)S(1)}, bf16[512,128]{1,0:T(8,128)(2,1)S(1)}, u32[]{:S(2)}, u32[]{:S(2)}) collective-permute-start(bf16[512,128]{1,0:T(8,128)(2,1)S(1)} %get-tuple-element.92), channel_id=1, source_target_pairs={{0,31},{1,2},{2,1},{3,4},{4,3},{5,6},{6,5},{7,8},{8,7},{9,10},{10,... | collective-permute-start | bytes 393224 | tf_op jit(solution)/shard_map/ppermute | solution.py:619
  112.4 9.2 %collective-permute-start.28 = (bf16[1024,128]{1,0:T(8,128)(2,1)S(1)}, bf16[1024,128]{1,0:T(8,128)(2,1)S(1)}, u32[]{:S(2)}, u32[]{:S(2)}) collective-permute-start(bf16[1024,128]{1,0:T(8,128)(2,1)S(1)} %shard_map.95), channel_id=1, source_target_pairs={{0,31},{1,2},{2,1},{3,4},{4,3},{5,6},{6,5},{7,8},{8,7},{9,10},{10,... | collective-permute-start | bytes 786440 | tf_op jit(solution)/shard_map/ppermute | solution.py:619
  115.8 10.5 %collective-permute-start.10 = (bf16[1536,128]{1,0:T(8,128)(2,1)S(1)}, bf16[1536,128]{1,0:T(8,128)(2,1)S(1)}, u32[]{:S(2)}, u32[]{:S(2)}) collective-permute-start(bf16[1536,128]{1,0:T(8,128)(2,1)S(1)} %get-tuple-element.71), channel_id=1, source_target_pairs={{0,31},{1,2},{2,1},{3,4},{4,3},{5,6},{6,5},{7,8},{8,7},{9,10},{10,... | collective-permute-start | bytes 1179656 | tf_op jit(solution)/shard_map/ppermute | solution.py:619
  117.5 8.8 %collective-permute-start.9 = (bf16[1536,128]{1,0:T(8,128)(2,1)S(1)}, bf16[1536,128]{1,0:T(8,128)(2,1)S(1)}, u32[]{:S(2)}, u32[]{:S(2)}) collective-permute-start(bf16[1536,128]{1,0:T(8,128)(2,1)S(1)} %get-tuple-element.71), channel_id=1, source_target_pairs={{0,1},{1,0},{2,3},{3,2},{4,5},{5,4},{6,7},{7,6},{8,9},{9,8},{10,11... | collective-permute-start | bytes 1179656 | tf_op jit(solution)/shard_map/ppermute | solution.py:614
  127.1 8.8 %collective-permute-start.30 = (bf16[512,128]{1,0:T(8,128)(2,1)S(1)}, bf16[512,128]{1,0:T(8,128)(2,1)S(1)}, u32[]{:S(2)}, u32[]{:S(2)}) collective-permute-start(bf16[512,128]{1,0:T(8,128)(2,1)S(1)} %shard_map.96.coarse_ref), channel_id=1, source_target_pairs={{0,31},{1,2},{2,1},{3,4},{4,3},{5,6},{6,5},{7,8},{8,7},{9,10},{10,... | collective-permute-start | bytes 393224 | tf_op jit(solution)/shard_map/ppermute | solution.py:619
  137.8 10.6 %collective-permute-start.33 = (bf16[1536,128]{1,0:T(8,128)(2,1)S(1)}, bf16[1536,128]{1,0:T(8,128)(2,1)S(1)}, u32[]{:S(2)}, u32[]{:S(2)}) collective-permute-start(bf16[1536,128]{1,0:T(8,128)(2,1)S(1)} %get-tuple-element.106), channel_id=1, source_target_pairs={{0,31},{1,2},{2,1},{3,4},{4,3},{5,6},{6,5},{7,8},{8,7},{9,10},{10,... | collective-permute-start | bytes 1179656 | tf_op jit(solution)/shard_map/ppermute | solution.py:619
  140.1 9.7 %collective-permute-start.32 = (bf16[512,128]{1,0:T(8,128)(2,1)S(1)}, bf16[512,128]{1,0:T(8,128)(2,1)S(1)}, u32[]{:S(2)}, u32[]{:S(2)}) collective-permute-start(bf16[512,128]{1,0:T(8,128)(2,1)S(1)} %get-tuple-element.105), channel_id=1, source_target_pairs={{0,31},{1,2},{2,1},{3,4},{4,3},{5,6},{6,5},{7,8},{8,7},{9,10},{10,... | collective-permute-start | bytes 393224 | tf_op jit(solution)/shard_map/ppermute | solution.py:619
  (13 other events, 75.5 us)
